TPU v7x, 128 devices: a whole 4x4x4 slice. The times are simulated.
128 devices in a mesh: replica: 32 (over y, x, z_lo), tensor: 4 (over z_hi, core).
Axes of the slice: x: 4, y: 4, z: 4 (z_hi: 2, z_lo: 2; z = z_hi * 2 + z_lo), core: 2. Of those that a mesh axis runs over, the one named last changes fastest.
Arguments:
- weight: bfloat16 [32, 4096, 2048], P('replica', None, 'tensor'), may hold values from -0.09375 to 0.09375
- momentum: bfloat16 [32, 4096, 2048], P('replica', None, 'tensor'), may hold values from -24 to 24
- inputs: bfloat16 [2, 16384, 4096], P(None, ('replica', 'tensor')), may hold values from -6 to 6
- out_grads: bfloat16 [2, 16384, 2048], P(None, 'replica', 'tensor'), may hold values from -6 to 6
Outputs:
- new_weight: bfloat16 [32, 4096, 2048], P('replica', None, 'tensor')
- new_momentum: bfloat16 [32, 4096, 2048], P('replica', None, 'tensor')
- input_grad: bfloat16 [2, 16384, 4096], P(None, ('replica', 'tensor'))
All inputs are finite; a program needn't handle non-finite values.
Results may differ from a plain program's by a relative error of at most 0.014.
Values may be sent and summed in bfloat16 or wider, within the bound.
A program may use at most 128 MiB of HBM per device.

v0:
```python
import jax
import jax.numpy as jnp
from jax import lax
from jax.sharding import PartitionSpec as P

learn_rate = 0.001
mom_decay = 0.9


def in_blocks(shard, dim, devices):
    dims = shard.shape
    blocks = shard.reshape(*dims[:dim], devices, dims[dim] // devices, *dims[dim + 1 :])
    return jnp.moveaxis(blocks, dim, 0)


def sum_at_owner(shard, axis, dim):
    blocks = in_blocks(shard, dim, lax.axis_size(axis))
    arrived = lax.all_to_all(blocks, axis, split_axis=0, concat_axis=0, tiled=True)
    return arrived.astype(jnp.float32).sum(axis=0)


def from_partner(block, axis, distance):
    count = lax.axis_size(axis)
    route = []
    for low in range(count):
        high = low | 1 << distance
        if high != low and high < count:
            route += [(low, high), (high, low)]
    return lax.ppermute(block, axis, route)


def silu_slope(pre):
    sigma = jax.nn.sigmoid(pre)
    return sigma * (1.0 + pre * (1.0 - sigma))


def input_partials(slope_grad, weight_now):
    partial_value = lax.dot_general(
        slope_grad, weight_now, (((1,), (1,)), ((), ())), preferred_element_type=jnp.float32
    )
    rounded = partial_value.astype(jnp.bfloat16)
    return sum_at_owner(rounded, "tensor", 0).astype(jnp.bfloat16)


def gossip_update(weight_now, moment_now, grad_w, step):
    moment_new = (mom_decay * moment_now.astype(jnp.float32) + grad_w).astype(jnp.bfloat16)
    stepped = (weight_now.astype(jnp.float32) - learn_rate * moment_new.astype(jnp.float32)).astype(
        jnp.bfloat16
    )
    other_weight, other_moment = from_partner((stepped, moment_new), "replica", step)
    averaged = ((stepped.astype(jnp.float32) + other_weight.astype(jnp.float32)) * 0.5).astype(
        jnp.bfloat16
    )
    moment_avg = ((moment_new.astype(jnp.float32) + other_moment.astype(jnp.float32)) * 0.5).astype(
        jnp.bfloat16
    )
    return (averaged, moment_avg)


def local(weight, momentum, inputs, out_grads):
    weight_now = weight[0]
    moment_now = momentum[0]
    grads_out = []
    for step in range(inputs.shape[0]):
        rows_here = inputs[step]
        gathered = lax.all_gather(rows_here, "tensor", axis=0, tiled=True)
        pre = jnp.dot(gathered, weight_now, preferred_element_type=jnp.float32)
        slope_grad = (out_grads[step].astype(jnp.float32) * silu_slope(pre)).astype(jnp.bfloat16)
        grad_w = lax.dot_general(
            gathered, slope_grad, (((0,), (0,)), ((), ())), preferred_element_type=jnp.float32
        )
        grads_out.append(input_partials(slope_grad, weight_now))
        next_weight, next_moment = gossip_update(weight_now, moment_now, grad_w, step)
        weight_now = next_weight
        moment_now = next_moment
    return (weight_now[None], moment_now[None], jnp.stack(grads_out))


def solution(mesh):
    return jax.shard_map(
        local,
        mesh=mesh,
        in_specs=(
            P("replica", None, "tensor"),
            P("replica", None, "tensor"),
            P(None, ("replica", "tensor"), None),
            P(None, "replica", "tensor"),
        ),
        out_specs=(
            P("replica", None, "tensor"),
            P("replica", None, "tensor"),
            P(None, ("replica", "tensor"), None),
        ),
        check_vma=False,
    )
```

profile of v0, /device:TPU:0, one launch (start us, length us, event | category | flops | bytes accessed | tf_op | source)
XLA Modules:
  0.0 492.5 jit_solution(18293548097176699641)
XLA Ops:
  7.2 3.2 fusion.48
  10.4 0.0 all-gather.7.cloned.1.call-start
  10.4 0.7 all-gather.7.cloned.1.call-update
  11.1 6.3 %copy.8 = bf16[1,4096,512]{1,2,0:T(8,128)(2,1)} copy(bf16[1,4096,512]{2,1,0:T(8,128)(2,1)} %param.5) | data formatting | bytes 8388608 | tf_op args[1]
  17.5 6.4 %copy.7 = bf16[1,4096,512]{1,2,0:T(8,128)(2,1)} copy(bf16[1,4096,512]{2,1,0:T(8,128)(2,1)} %param.4) | data formatting | bytes 8388608 | tf_op args[0]
  23.9 27.8 %all-gather.5.cloned.1.call-done = bf16[1,512,4096]{2,1,0:T(8,128)(2,1)} async-done(((bf16[1,128,4096]{2,1,0:T(8,128)(2,1)}), bf16[1,512,4096]{2,1,0:T(8,128)(2,1)}) %all-gather.5.cloned.1.call-update) | async-done | bytes 4194320 | tf_op jit(solution)/shard_map/all_gather | solution.py:66
  51.7 5.9 %fusion.13 = f32[512,512]{1,0:T(8,128)S(1)} fusion(bf16[1,4096,512]{2,1,0:T(8,128)(2,1)} %param.4, bf16[1,512,4096]{2,1,0:T(8,128)(2,1)} %all-gather.5.cloned.1.call-done), kind=kOutput, calls=%fused_computation.23 | convolution fusion | flops 2147483648 | bytes 9437184 | tf_op jit(solution)/shard_map/dot_general | solution.py:67
  57.6 1.2 copy-done.4
  58.8 6.5 %fusion.1 = (bf16[4096,512]{0,1:T(8,128)(2,1)}, bf16[4096,512]{0,1:T(8,128)(2,1)}) fusion(bf16[1,4096,512]{1,2,0:T(8,128)(2,1)S(1)} %copy-done.2, bf16[1,512,4096]{2,1,0:T(8,128)(2,1)S(1)} %copy-done.4, f32[512,512]{1,0:T(8,128)S(1)} %fusion.13, bf16[2,512,512]{2,1,0:T(8,128)(2,1)S(1)} %copy-done.5, bf16[1,4096,512]{1,2,0:T(8,128)(2,1)S(1)} %copy-done.1), kind=kOutput, calls=%fused_computation.5 | convolution fusion | flops 2168979456 | bytes 22544384 | tf_op jit(solution)/shard_map/dot_general | solution.py:69
  65.3 0.5 collective-permute-start
  65.8 1.5 collective-permute-start.1
  67.4 46.2 %all-gather.7.cloned.1.call-done = bf16[1,512,4096]{2,1,0:T(8,128)(2,1)} async-done(((bf16[1,128,4096]{2,1,0:T(8,128)(2,1)}), bf16[1,512,4096]{2,1,0:T(8,128)(2,1)}) %all-gather.7.cloned.1.call-update) | async-done | bytes 4194320 | tf_op jit(solution)/shard_map/all_gather | solution.py:66
  113.5 65.3 %collective-permute-done = bf16[4096,512]{0,1:T(8,128)(2,1)} collective-permute-done((bf16[4096,512]{0,1:T(8,128)(2,1)}, bf16[4096,512]{0,1:T(8,128)(2,1)}, u32[]{:S(2)}, u32[]{:S(2)}) %collective-permute-start) | collective-permute-done | bytes 4194336 | tf_op jit(solution)/shard_map/ppermute | solution.py:29
  178.8 7.0 %fusion.23 = f32[512,512]{1,0:T(8,128)S(1)} fusion(bf16[1,512,4096]{2,1,0:T(8,128)(2,1)} %all-gather.7.cloned.1.call-done, bf16[4096,512]{0,1:T(8,128)(2,1)} %collective-permute-done, bf16[4096,512]{0,1:T(8,128)(2,1)} %get-tuple-element.10), kind=kOutput, calls=%fused_computation.32 | convolution fusion | flops 2157969408 | bytes 13631488 | tf_op jit(solution)/shard_map/dot_general | solution.py:67
  185.9 82.6 %collective-permute-done.1 = bf16[4096,512]{0,1:T(8,128)(2,1)} collective-permute-done((bf16[4096,512]{0,1:T(8,128)(2,1)}, bf16[4096,512]{0,1:T(8,128)(2,1)}, u32[]{:S(2)}, u32[]{:S(2)}) %collective-permute-start.1) | collective-permute-done | bytes 4194336 | tf_op jit(solution)/shard_map/ppermute | solution.py:29
  268.5 9.2 %fusion.8 = bf16[4096,512]{0,1:T(8,128)(2,1)} fusion(bf16[4096,512]{0,1:T(8,128)(2,1)} %collective-permute-done.1, bf16[4096,512]{0,1:T(8,128)(2,1)} %get-tuple-element.11, bf16[1,512,4096]{2,1,0:T(8,128)(2,1)S(1)} %copy-done.3, f32[512,512]{1,0:T(8,128)S(1)} %fusion.23, bf16[2,512,512]{2,1,0:T(8,128)(2,1)S(1)} %copy-done.5), kind=kOutput, calls=%fused_computation.13 | convolution fusion | flops 2168979456 | bytes 18350080 | tf_op jit(solution)/shard_map/dot_general | solution.py:69
  277.7 1.5 collective-permute-start.3
  279.2 4.5 convolution_convert_fusion.1
  283.7 4.9 all-to-all-start
  288.6 81.8 %collective-permute-done.3 = bf16[4096,512]{0,1:T(8,128)(2,1)} collective-permute-done((bf16[4096,512]{0,1:T(8,128)(2,1)}, bf16[4096,512]{0,1:T(8,128)(2,1)}, u32[]{:S(2)}, u32[]{:S(2)}) %collective-permute-start.3) | collective-permute-done | bytes 4194336 | tf_op jit(solution)/shard_map/ppermute | solution.py:29
  370.4 9.9 %fusion.11 = (bf16[1,4096,512]{1,2,0:T(8,128)(2,1)}, bf16[4096,512]{0,1:T(8,128)(2,1)}) fusion(bf16[4096,512]{0,1:T(8,128)(2,1)} %collective-permute-done.3, bf16[4096,512]{0,1:T(8,128)(2,1)} %fusion.8, bf16[4096,512]{0,1:T(8,128)(2,1)} %collective-permute-done, bf16[4096,512]{0,1:T(8,128)(2,1)} %get-tuple-element.10), kind=kLoop, calls=%fused_computation.21 | loop fusion | flops 29360128 | bytes 25165824 | tf_op jit(solution)/shard_map/broadcast_in_dim | solution.py:76
  380.2 1.5 collective-permute-start.2
  381.7 8.2 %convolution_convert_fusion = bf16[512,4096]{1,0:T(8,128)(2,1)} fusion(f32[512,512]{1,0:T(8,128)S(1)} %fusion.23, bf16[2,512,512]{2,1,0:T(8,128)(2,1)S(1)} %copy-done.5, bf16[4096,512]{0,1:T(8,128)(2,1)} %collective-permute-done, bf16[4096,512]{0,1:T(8,128)(2,1)} %get-tuple-element.10), kind=kOutput, calls=%fused_computation.18 | convolution fusion | flops 2162688000 | bytes 14155776 | tf_op jit(solution)/shard_map/dot_general | solution.py:38
  389.9 4.9 all-to-all-start.1
  394.8 3.1 reduce_sum.24
  397.8 46.7 %all-to-all-done.1 = bf16[4,128,4096]{2,1,0:T(8,128)(2,1)} async-done(((bf16[4,128,4096]{2,1,0:T(8,128)(2,1)}), bf16[4,128,4096]{2,1,0:T(8,128)(2,1)}, u32[]{:S(2)}, u32[]{:S(2)}) %all-to-all-start.1) | async-done | bytes 4194336 | tf_op jit(solution)/shard_map/all_to_all | solution.py:18
  444.5 3.1 reduce_sum.25
  447.6 1.5 pad_maximum_fusion
  449.1 6.4 %copy.11 = bf16[1,4096,512]{2,1,0:T(8,128)(2,1)} copy(bf16[1,4096,512]{1,2,0:T(8,128)(2,1)} %get-tuple-element.6) | data formatting | bytes 8388608
  455.5 16.6 %collective-permute-done.2 = bf16[4096,512]{0,1:T(8,128)(2,1)} collective-permute-done((bf16[4096,512]{0,1:T(8,128)(2,1)}, bf16[4096,512]{0,1:T(8,128)(2,1)}, u32[]{:S(2)}, u32[]{:S(2)}) %collective-permute-start.2) | collective-permute-done | bytes 4194336 | tf_op jit(solution)/shard_map/ppermute | solution.py:29
  472.0 7.2 %fusion.10 = bf16[1,4096,512]{1,2,0:T(8,128)(2,1)} fusion(bf16[4096,512]{0,1:T(8,128)(2,1)} %collective-permute-done.2, bf16[4096,512]{0,1:T(8,128)(2,1)} %get-tuple-element.7), kind=kLoop, calls=%fused_computation.20 | loop fusion | flops 10485760 | bytes 12582912 | tf_op jit(solution)/shard_map/broadcast_in_dim | solution.py:76
  479.2 6.4 %copy.10 = bf16[1,4096,512]{2,1,0:T(8,128)(2,1)} copy(bf16[1,4096,512]{1,2,0:T(8,128)(2,1)} %fusion.10) | data formatting | bytes 8388608
  (14 shorter events, 0.1 us)
Async XLA Ops:
  7.2 44.5 %all-gather.5.cloned.1.call-start = ((), (), s32[]{:S(2)}) async-start(), calls=%async_computation.2 | async-start | bytes 5242880 | tf_op jit(solution)/shard_map/all_gather | solution.py:66
  10.4 103.1 %all-gather.7.cloned.1.call-start = ((), (), s32[]{:S(2)}) async-start(), calls=%async_computation.3 | async-start | bytes 5242880 | tf_op jit(solution)/shard_map/all_gather | solution.py:66
  23.8 33.8 %copy-start.5 = (bf16[2,512,512]{2,1,0:T(8,128)(2,1)S(1)}, bf16[2,512,512]{2,1,0:T(8,128)(2,1)}, u32[]{:S(2)}) copy-start(bf16[2,512,512]{2,1,0:T(8,128)(2,1)} %param.7) | copy-start | bytes 3145732
  51.7 5.9 %copy-start.1 = (bf16[1,4096,512]{1,2,0:T(8,128)(2,1)S(1)}, bf16[1,4096,512]{1,2,0:T(8,128)(2,1)}, u32[]{:S(2)}) copy-start(bf16[1,4096,512]{1,2,0:T(8,128)(2,1)} %copy.8) | copy-start | bytes 12582916
  51.7 5.9 %copy-start.2 = (bf16[1,4096,512]{1,2,0:T(8,128)(2,1)S(1)}, bf16[1,4096,512]{1,2,0:T(8,128)(2,1)}, u32[]{:S(2)}) copy-start(bf16[1,4096,512]{1,2,0:T(8,128)(2,1)} %copy.7) | copy-start | bytes 12582916
  51.7 7.1 %copy-start.4 = (bf16[1,512,4096]{2,1,0:T(8,128)(2,1)S(1)}, bf16[1,512,4096]{2,1,0:T(8,128)(2,1)}, u32[]{:S(2)}) copy-start(bf16[1,512,4096]{2,1,0:T(8,128)(2,1)} %all-gather.5.cloned.1.call-done) | copy-start | bytes 12582916
  65.3 113.5 %collective-permute-start = (bf16[4096,512]{0,1:T(8,128)(2,1)}, bf16[4096,512]{0,1:T(8,128)(2,1)}, u32[]{:S(2)}, u32[]{:S(2)}) collective-permute-start(bf16[4096,512]{0,1:T(8,128)(2,1)} %get-tuple-element.10), channel_id=1, source_target_pairs={{0,4},{4,0},{8,12},{12,8},{16,20},{20,16},{24,28},{28,24},{32,36},... | collective-permute-start | bytes 12582920 | tf_op jit(solution)/shard_map/ppermute | solution.py:29
  65.8 202.6 %collective-permute-start.1 = (bf16[4096,512]{0,1:T(8,128)(2,1)}, bf16[4096,512]{0,1:T(8,128)(2,1)}, u32[]{:S(2)}, u32[]{:S(2)}) collective-permute-start(bf16[4096,512]{0,1:T(8,128)(2,1)} %get-tuple-element.11), channel_id=1, source_target_pairs={{0,4},{4,0},{8,12},{12,8},{16,20},{20,16},{24,28},{28,24},{32,36},... | collective-permute-start | bytes 12582920 | tf_op jit(solution)/shard_map/ppermute | solution.py:29
  113.5 155.0 %copy-start.3 = (bf16[1,512,4096]{2,1,0:T(8,128)(2,1)S(1)}, bf16[1,512,4096]{2,1,0:T(8,128)(2,1)}, u32[]{:S(2)}) copy-start(bf16[1,512,4096]{2,1,0:T(8,128)(2,1)} %all-gather.7.cloned.1.call-done) | copy-start | bytes 12582916
  185.9 93.3 %copy-start = (bf16[1,4096,512]{2,1,0:T(8,128)(2,1)S(1)}, bf16[1,4096,512]{2,1,0:T(8,128)(2,1)}, u32[]{:S(2)}) copy-start(bf16[1,4096,512]{2,1,0:T(8,128)(2,1)} %param.4) | copy-start | bytes 12582916
  277.7 92.7 %collective-permute-start.3 = (bf16[4096,512]{0,1:T(8,128)(2,1)}, bf16[4096,512]{0,1:T(8,128)(2,1)}, u32[]{:S(2)}, u32[]{:S(2)}) collective-permute-start(bf16[4096,512]{0,1:T(8,128)(2,1)} %fusion.8), channel_id=1, source_target_pairs={{0,8},{8,0},{4,12},{12,4},{16,24},{24,16},{20,28},{28,20},{32,40},... | collective-permute-start | bytes 12582920 | tf_op jit(solution)/shard_map/ppermute | solution.py:29
  283.7 106.2 %all-to-all-start = ((bf16[4,128,4096]{2,1,0:T(8,128)(2,1)}), bf16[4,128,4096]{2,1,0:T(8,128)(2,1)}, u32[]{:S(2)}, u32[]{:S(2)}) async-start(bf16[4,128,4096]{2,1,0:T(8,128)(2,1)} %bitcast.66), calls=%async_computation | async-start | bytes 8388608 | tf_op jit(solution)/shard_map/all_to_all | solution.py:18
  380.2 91.8 %collective-permute-start.2 = (bf16[4096,512]{0,1:T(8,128)(2,1)}, bf16[4096,512]{0,1:T(8,128)(2,1)}, u32[]{:S(2)}, u32[]{:S(2)}) collective-permute-start(bf16[4096,512]{0,1:T(8,128)(2,1)} %get-tuple-element.7), channel_id=1, source_target_pairs={{0,8},{8,0},{4,12},{12,4},{16,24},{24,16},{20,28},{28,20},{32,40},... | collective-permute-start | bytes 12582920 | tf_op jit(solution)/shard_map/ppermute | solution.py:29
  389.9 54.6 %all-to-all-start.1 = ((bf16[4,128,4096]{2,1,0:T(8,128)(2,1)}), bf16[4,128,4096]{2,1,0:T(8,128)(2,1)}, u32[]{:S(2)}, u32[]{:S(2)}) async-start(bf16[4,128,4096]{2,1,0:T(8,128)(2,1)} %bitcast.67), calls=%async_computation.1 | async-start | bytes 8388608 | tf_op jit(solution)/shard_map/all_to_all | solution.py:18
Sparse Core Ops, SparseCore 0:
  10.5 41.1 all-gather.4
  53.9 59.5 all-gather.6
where the time goes:
time: 493 us; the launch traced here: 492 us
  waiting for transfers between devices  368 us (75%)
  matrix products  41.4 us (8%)
  local copies, waits for them, and re-layouts  29.8 us (6%)
  other arithmetic  24.7 us (5%)
  starting transfers between devices  14.8 us (3%)
  between operations  14.1 us (3%)
    ppermute x4, waiting for transfers between devices, from_partner(): return lax.ppermute(block, axis, route)  246 us
    all_gather x2, waiting for transfers between devices, local(): gathered = lax.all_gather(rows_here, 'tensor', axis=0, tiled=True)  74 us
    all_to_all x2, waiting for transfers between devices, sum_at_owner(): lax.all_to_all(blocks, axis, split_axis=0, concat_axis=0, tiled=True)  46.7 us
    unnamed x16, local copies, waits for them, and re-layouts  26.7 us
    broadcast_in_dim x2, other arithmetic, local(): return (weight_now[None], moment_now[None], jnp.stack(grads_out))  17 us
    dot_general x2, matrix products, local(): lax.dot_general(gathered, slope_grad, (((0,), (0,)), ((), ())), preferred...  15.7 us
    dot_general x2, matrix products, local(): pre = jnp.dot(gathered, weight_now, preferred_element_type=jnp.float32)  13 us
    dot_general x2, matrix products, input_partials(): lax.dot_general(slope_grad, weight_now, (((1,), (1,)), ((), ())), preferr...  12.7 us
  transfers between devices with their start and end apart: 8, of which 7 were waited for; matrix products, arithmetic and copies ran while one was open for 14% of the time, Pallas kernels for 0%

commit v1 on v0

v1 whole, which is shorter than its diff:
```python
import jax
import jax.numpy as jnp
from jax import lax
from jax.experimental import pallas as pl
from jax.experimental.pallas import tpu as pltpu
from jax.sharding import PartitionSpec as P

learn_rate = 0.001
mom_decay = 0.9

bf16 = jnp.bfloat16
f32 = jnp.float32

CHUNKS = 4
TRANSFERS = (
    "x0n", "x0f", "x0c0", "x0fn", "x0nf", "x0c1", "x1n", "x1f", "x1c", "x1fn", "x1nf", "x1c1",
    "xbc", "xca", "xcb", "xcc", "q", "s1n", "s1x", "s1c", "s1bc", "st", "p0c", "a0f", "a0n", "a0fn",
    "a0nf", "a1n", "a1f", "to_near", "to_far",
)
NUMBER = {name: k for k, name in enumerate(TRANSFERS)}
CHAINS = {name: len(TRANSFERS) + CHUNKS * k for k, name in enumerate(("w1", "w2", "w3", "m1", "m2", "m3"))}
COPIES = len(TRANSFERS) + CHUNKS * len(CHAINS)


def silu_slope(pre):
    sigma = jax.nn.sigmoid(pre)
    return sigma * (1.0 + pre * (1.0 - sigma))


def dot(a, b, left, right):
    return lax.dot_general(a, b, (((left,), (right,)), ((), ())), preferred_element_type=f32)


def kernel(
    w_hbm, m_hbm, x_hbm, og_hbm, new_w, new_m, grad_in,
    wv, mv, stepped, stepped_o, x0, xa, xb, xc, lw1, lw2, lw3, lm1, lm2, lm3,
    tn, tf, lp0, t0n, t0f, r0n, r0f, t1n, t1f, r1n, r1f,
    q_own, q_give, q_got, og, s0, s1, s1b, s1c, s1o, s1bo,
    send, recv, local,
):
    d, cols = wv.shape
    rows = x0.shape[0] // 4
    cut = rows // 2
    half = d // 2
    chunk = half // CHUNKS
    tile = chunk // 2
    pair = 2 * rows
    n = 4 * rows

    r = lax.axis_index("replica")
    t = lax.axis_index("tensor")
    lower = (r // 2) % 2
    keep0 = lower * half
    give0 = (1 - lower) * half
    r_near = r + 1 - 2 * (r % 2)
    t_core = t + 1 - 2 * (t % 2)
    t_far = (t + 2) % 4
    core = (r, t_core)
    near = (r_near, t)
    far = (r_near, t_far)
    across = (r + 2 - 4 * lower, t)

    barrier = pltpu.get_barrier_semaphore()
    for there in (core, near, far, across):
        pl.semaphore_signal(barrier, inc=1, device_id=there, device_id_type=pl.DeviceIdType.MESH)
    pl.semaphore_wait(barrier, 4)

    def piece(start, size):
        return pl.ds(pl.multiple_of(start, size), size)

    def remote(k, src, dst, there):
        return pltpu.make_async_remote_copy(
            src_ref=src, dst_ref=dst, send_sem=send.at[k], recv_sem=recv.at[k],
            device_id=there, device_id_type=pl.DeviceIdType.MESH,
        )

    routes = {
        "x0n": (x_hbm.at[0, pl.ds(cut, cut)], tn, near),
        "x0f": (x_hbm.at[0, pl.ds(0, cut)], tf, far),
        "x0c0": (x_hbm.at[0], x0.at[pl.ds(pair, rows)], core),
        "x0fn": (tf, x0.at[pl.ds(rows, cut)], near),
        "x0nf": (tn, x0.at[pl.ds(rows + cut, cut)], far),
        "x0c1": (x0.at[pl.ds(rows, rows)], x0.at[pl.ds(pair + rows, rows)], core),
        "x1n": (x_hbm.at[1], xb.at[pl.ds(0, rows)], near),
        "x1f": (x_hbm.at[1], xb.at[pl.ds(rows, rows)], far),
        "x1c": (x_hbm.at[1], xa.at[pl.ds(pair, rows)], core),
        "x1fn": (xb.at[pl.ds(rows, cut)], xa.at[pl.ds(rows, cut)], near),
        "x1nf": (xb.at[pl.ds(cut, cut)], xa.at[pl.ds(rows + cut, cut)], far),
        "x1c1": (xa.at[pl.ds(rows, rows)], xa.at[pl.ds(pair + rows, rows)], core),
        "xbc": (xb.at[pl.ds(0, pair)], xb.at[pl.ds(pair, pair)], core),
        "xca": (x_hbm.at[1], xc.at[pl.ds(0, rows)], across),
        "xcb": (xa.at[pl.ds(rows, rows)], xc.at[pl.ds(rows, rows)], across),
        "xcc": (xc.at[pl.ds(0, pair)], xc.at[pl.ds(pair, pair)], core),
        "q": (q_give, q_got, near),
        "s1n": (s1, s1b, near),
        "s1x": (s1, s1c, across),
        "s1c": (s1.at[pl.ds(pair, pair)], s1o, core),
        "s1bc": (s1b.at[pl.ds(pair, pair)], s1bo, core),
        "st": (stepped, stepped_o, core),
        "p0c": (x0.at[pl.ds(pair, pair)], lp0, core),
        "a0f": (lp0.at[pl.ds(rows, cut)], t0f, far),
        "a0n": (lp0.at[pl.ds(rows + cut, cut)], t0n, near),
        "a0fn": (t0f, r0n, near),
        "a0nf": (t0n, r0f, far),
        "a1n": (xb.at[pl.ds(rows, cut)], t1n, near),
        "a1f": (xb.at[pl.ds(rows + cut, cut)], t1f, far),
        "to_near": (xb.at[pl.ds(pair, rows)], r1n, near),
        "to_far": (xb.at[pl.ds(pair + rows, rows)], r1f, far),
    }

    def copy(name):
        return remote(NUMBER[name], *routes[name])

    def go(*names):
        for name in names:
            copy(name).start()

    def arrived(*names):
        for name in names:
            copy(name).wait_recv()

    def sent(*names):
        for name in names:
            copy(name).wait_send()

    def link(name, i):
        here = piece(i * chunk, chunk)
        give = piece(give0 + i * chunk, chunk)
        src, dst, there = {
            "w1": (w_hbm.at[0, give], lw1.at[here], across),
            "w2": (lw1.at[here], lw2.at[here], near),
            "w3": (lw2.at[here], lw3.at[here], across),
            "m1": (mv.at[give], lm1.at[here], across),
            "m2": (lm1.at[here], lm2.at[here], near),
            "m3": (lm2.at[here], lm3.at[here], across),
        }[name]
        return remote(CHAINS[name] + i, src, dst, there)

    def load(k, src, dst):
        return pltpu.make_async_copy(src, dst, local.at[k])

    loads = [
        load(0, x_hbm.at[0], x0.at[pl.ds(0, rows)]),
        load(1, w_hbm.at[0], wv),
        load(2, og_hbm, og),
        load(3, x_hbm.at[1], xa.at[pl.ds(0, rows)]),
        load(4, m_hbm.at[0], mv),
    ]

    def each(count, body):
        @pl.loop(0, count)
        def _(i):
            body(i)

    loads[0].start()
    go("x0f", "x0n", "x0c0")
    loads[1].start()
    loads[2].start()
    each(CHUNKS, lambda i: link("w1", i).start())
    loads[4].start()
    loads[3].start()
    arrived("x0f")
    go("x0fn")
    arrived("x0n")
    go("x0nf", "x1n", "x1f", "x1c")
    arrived("x0fn", "x0nf")
    go("x0c1")
    loads[0].wait()
    loads[1].wait()
    loads[2].wait()
    arrived("x0c0", "x0c1")

    depth = d // 8

    def product(out, lhs, rhs):
        out[...] = jnp.zeros_like(out)

        def add(k):
            here = piece(k * depth, depth)
            out[...] += dot(lhs[:, here], rhs[here, :], 1, 0)

        each(d // depth, add)

    def slopes(out, step, pre):
        for j, block in enumerate((t, t_far, t_core, (t_core + 2) % 4)):
            up = og[step, piece(block * rows, rows), :].astype(f32)
            here = pl.ds(j * rows, rows)
            out[here, :] = (up * silu_slope(pre(here))).astype(bf16)

    product(q_own, x0, wv)
    slopes(s0, 0, lambda here: q_own[here, :])
    loads[4].wait()

    def moment_tile(start):
        here = piece(start, tile)
        grad = dot(x0[:, here], s0[...], 0, 0)
        moment = (mom_decay * mv[here, :].astype(f32) + grad).astype(bf16)
        mv[here, :] = moment
        stepped[here, :] = (wv[here, :].astype(f32) - learn_rate * moment.astype(f32)).astype(bf16)

    def moment_chunk(i):
        moment_tile(give0 + i * chunk)
        moment_tile(give0 + i * chunk + tile)
        link("m1", i).start()

    each(CHUNKS, moment_chunk)
    each(half // tile, lambda i: moment_tile(keep0 + i * tile))
    go("st")

    arrived("x1f")
    go("x1fn")
    arrived("x1n")
    go("x1nf")

    sent("x0c1")

    def part0(first):
        def one(k):
            here = piece(k * tile, tile)
            x0[pl.ds(first, pair), here] = dot(s0[pl.ds(first, pair), :], wv[here, :], 1, 1).astype(bf16)

        each(d // tile, one)

    part0(pair)
    go("p0c")
    part0(0)

    def pair_chunk(own, landed, first, second, i):
        link(first, i).wait_recv()
        here = piece(i * chunk, chunk)
        mine = own[piece(keep0 + i * chunk, chunk), :].astype(f32)
        landed[here, :] = ((mine + landed[here, :].astype(f32)) * 0.5).astype(bf16)
        link(second, i).start()

    def mean_chunk(landed, other, second, third, i):
        link(second, i).wait_recv()
        here = piece(i * chunk, chunk)
        other[here, :] = ((landed[here, :].astype(f32) + other[here, :].astype(f32)) * 0.5).astype(bf16)
        link(third, i).start()

    each(CHUNKS // 2, lambda i: pair_chunk(wv, lw1, "w1", "w2", i))

    loads[3].wait()
    arrived("x1fn", "x1nf")
    go("x1c1", "xbc")
    arrived("p0c")
    lp0[pl.ds(rows, rows), :] = (
        x0[pl.ds(rows, rows), :].astype(f32) + lp0[pl.ds(rows, rows), :].astype(f32)
    ).astype(bf16)
    go("a0f", "a0n")

    arrived("x1c", "x1c1", "xbc")
    product(q_give, xb, stepped)
    go("q")
    product(q_own, xa, stepped)
    go("xca")
    arrived("a0f")
    go("a0fn")
    arrived("a0n")
    go("a0nf")
    each(CHUNKS // 2, lambda i: pair_chunk(wv, lw1, "w1", "w2", i + CHUNKS // 2))
    arrived("q")
    slopes(s1, 1, lambda here: (q_own[here, :] + q_got[here, :]) * 0.5)
    go("s1c", "s1n", "s1x", "xcb")
    each(CHUNKS, lambda i: pair_chunk(mv, lm1, "m1", "m2", i))
    arrived("s1n")
    go("s1bc")
    arrived("s1c", "s1bc", "st")

    sent("x1fn", "x1nf", "xbc")

    def part1(k):
        here = piece(k * tile, tile)
        mine = jnp.concatenate([s1[pl.ds(0, pair), :], s1b[pl.ds(0, pair), :]], axis=0)
        theirs = jnp.concatenate([s1o[...], s1bo[...]], axis=0)
        both = dot(mine, stepped[here, :], 1, 1) + dot(theirs, stepped_o[here, :], 1, 1)
        xb[:, here] = (both * 0.5).astype(bf16)

    each(d // tile, part1)
    go("a1n", "a1f")

    each(CHUNKS, lambda i: mean_chunk(lw1, lw2, "w2", "w3", i))
    arrived("a1n")
    here = pl.ds(pair + rows, cut)
    xb[here, :] = (xb[here, :].astype(f32) + t1n[...].astype(f32)).astype(bf16)
    go("to_far")
    arrived("a1f")
    here = pl.ds(pair + cut, cut)
    xb[here, :] = (xb[here, :].astype(f32) + t1f[...].astype(f32)).astype(bf16)
    go("to_near")
    arrived("xca", "xcb")
    go("xcc")
    each(CHUNKS, lambda i: mean_chunk(lm1, lm2, "m2", "m3", i))

    arrived("a0fn", "a0nf")
    for k, back in enumerate((r0n, r0f)):
        here = pl.ds(k * cut, cut)
        x0[here, :] = (
            x0[here, :].astype(f32) + lp0[here, :].astype(f32) + back[...].astype(f32)
        ).astype(bf16)
    load(0, x0.at[pl.ds(0, rows)], grad_in.at[0]).start()

    arrived("s1x", "xcc")
    each(CHUNKS, lambda i: link("m1", i).wait_send())

    def finish(w_mean, m_mean, start, i):
        from_ = piece(i * tile, tile)
        here = piece(start + i * tile, tile)
        grad = dot(xa[:, here], s1[...], 0, 0) + dot(xc[:, here], s1c[...], 0, 0)
        m_now = m_mean[from_, :].astype(f32)
        moment = (mom_decay * m_now + grad * 0.5).astype(bf16)
        mv[here, :] = moment
        wv[here, :] = (
            w_mean[from_, :].astype(f32) - learn_rate * (m_now + moment.astype(f32))
        ).astype(bf16)

    each(half // tile, lambda i: finish(lw2, lm2, keep0, i))
    load(1, wv.at[piece(keep0, half)], new_w.at[0, piece(keep0, half)]).start()
    load(2, mv.at[piece(keep0, half)], new_m.at[0, piece(keep0, half)]).start()

    arrived("to_near", "to_far")
    x_first = xb[pl.ds(0, rows), :].astype(f32)
    xb[pl.ds(0, rows), :] = (x_first + r1n[...].astype(f32) + r1f[...].astype(f32)).astype(bf16)
    load(3, xb.at[pl.ds(0, rows)], grad_in.at[1]).start()

    def last_w(i):
        there = piece(give0 + i * chunk, chunk)
        return load(5 + i, wv.at[there], new_w.at[0, there])

    def last_m(i):
        there = piece(give0 + i * chunk, chunk)
        return load(5 + CHUNKS + i, mv.at[there], new_m.at[0, there])

    def finish_chunk(i):
        link("w3", i).wait_recv()
        link("m3", i).wait_recv()
        finish(lw3, lm3, give0, 2 * i)
        finish(lw3, lm3, give0, 2 * i + 1)
        last_w(i).start()
        last_m(i).start()

    each(CHUNKS, finish_chunk)

    sent(*[name for name in TRANSFERS if name not in ("x0c1", "x1fn", "x1nf", "xbc")])

    def drain(i):
        for name in ("w1", "w2", "w3", "m2", "m3"):
            link(name, i).wait_send()
        last_w(i).wait()
        last_m(i).wait()

    each(CHUNKS, drain)
    load(0, x0.at[pl.ds(0, rows)], grad_in.at[0]).wait()
    load(1, wv.at[piece(keep0, half)], new_w.at[0, piece(keep0, half)]).wait()
    load(2, mv.at[piece(keep0, half)], new_m.at[0, piece(keep0, half)]).wait()
    load(3, xb.at[pl.ds(0, rows)], grad_in.at[1]).wait()


def local(weight, momentum, inputs, out_grads):
    d, cols = weight.shape[1:]
    rows = inputs.shape[1]
    n, pair, cut, half = 4 * rows, 2 * rows, rows // 2, d // 2
    full = (d, cols)
    vmem = (
        [(full, bf16)] * 4
        + [((n, d), bf16)] * 4
        + [((half, cols), bf16)] * 6
        + [((cut, d), bf16)] * 2
        + [((pair, d), bf16)]
        + [((cut, d), bf16)] * 6
        + [((rows, d), bf16)] * 2
        + [((n, cols), f32)] * 3
        + [((2, n, cols), bf16)]
        + [((n, cols), bf16)] * 4
        + [((pair, cols), bf16)] * 2
    )
    return pl.pallas_call(
        kernel,
        out_shape=(
            jax.ShapeDtypeStruct(weight.shape, bf16),
            jax.ShapeDtypeStruct(momentum.shape, bf16),
            jax.ShapeDtypeStruct(inputs.shape, bf16),
        ),
        in_specs=[pl.BlockSpec(memory_space=pl.ANY)] * 4,
        out_specs=[pl.BlockSpec(memory_space=pl.ANY)] * 3,
        scratch_shapes=[pltpu.VMEM(shape, kind) for shape, kind in vmem]
        + [
            pltpu.SemaphoreType.DMA((COPIES,)),
            pltpu.SemaphoreType.DMA((COPIES,)),
            pltpu.SemaphoreType.DMA((5 + 2 * CHUNKS,)),
        ],
        compiler_params=pltpu.CompilerParams(
            collective_id=0, has_side_effects=True, vmem_limit_bytes=63 << 20
        ),
    )(weight, momentum, inputs, out_grads)


def solution(mesh):
    return jax.shard_map(
        local,
        mesh=mesh,
        in_specs=(
            P("replica", None, "tensor"),
            P("replica", None, "tensor"),
            P(None, ("replica", "tensor"), None),
            P(None, "replica", "tensor"),
        ),
        out_specs=(
            P("replica", None, "tensor"),
            P("replica", None, "tensor"),
            P(None, ("replica", "tensor"), None),
        ),
        check_vma=False,
    )
```

time: 493 us -> 280 us (0.57)
  waiting for transfers between devices: 368 us -> 0 us
  Pallas kernels: 0 us -> 270 us
  matrix products: 41.4 us -> 0 us
  other arithmetic: 24.7 us -> 0 us
  local copies, waits for them, and re-layouts: 29.8 us -> 9.06 us
  starting transfers between devices: 14.8 us -> 0 us
  between operations: 14.1 us -> 0.65 us
    pallas_call x0 -> x1, Pallas kernels: none -> 270 us  [local(): pl.pallas_call(kernel, out_shape=(jax.ShapeDtypeStruct(weight.shape, bf16...]
    ppermute x4 -> x0, waiting for transfers between devices: 246 us -> none  [from_partner(): return lax.ppermute(block, axis, route)]
    all_gather x2 -> x0, waiting for transfers between devices: 74 us -> none  [local(): gathered = lax.all_gather(rows_here, 'tensor', axis=0, tiled=True)]
    all_to_all x2 -> x0, waiting for transfers between devices: 46.7 us -> none  [sum_at_owner(): lax.all_to_all(blocks, axis, split_axis=0, concat_axis=0, tiled=True)]
    dot_general x6 -> x0, matrix products: 41.4 us -> none  [the longest x2 15.7 us: local(): lax.dot_general(gathered, slope_grad, (((0,), (0,)), ((), ())), preferred...]
    unnamed x16 -> x7, local copies, waits for them, and re-layouts: 26.7 us -> 9.06 us
    broadcast_in_dim x2 -> x0, other arithmetic: 17 us -> none  [local(): return (weight_now[None], moment_now[None], jnp.stack(grads_out))]
    all_to_all x2 -> x0, starting transfers between devices: 9.76 us -> none  [sum_at_owner(): lax.all_to_all(blocks, axis, split_axis=0, concat_axis=0, tiled=True)]
  transfers between devices with their start and end apart: 8 -> 0, of which waited for: 7 -> 0; matrix products, arithmetic and copies ran while one was open for 14% -> 0% of each run, Pallas kernels for 0% -> 0%
where the time goes in v1:
time: 280 us
  Pallas kernels  270 us (96%)
  local copies, waits for them, and re-layouts  9.06 us (3%)
    pallas_call x1, Pallas kernels, local(): pl.pallas_call(kernel, out_shape=(jax.ShapeDtypeStruct(weight.shape, bf16...  270 us
    unnamed x7, local copies, waits for them, and re-layouts  9.06 us

profile of v1, /device:TPU:0, one launch (start us, length us, event | category | flops | bytes accessed | tf_op | source)
XLA Modules:
  0.0 279.8 jit_solution(1298908710822347135)
XLA Ops:
  0.6 270.1 %shard_map.67 = (bf16[1,4096,512]{2,1,0:T(8,128)(2,1)}, bf16[1,4096,512]{2,1,0:T(8,128)(2,1)}, bf16[2,128,4096]{2,1,0:T(8,128)(2,1)}) custom-call(bf16[1,4096,512]{2,1,0:T(8,128)(2,1)} %w_hbm.1, bf16[1,4096,512]{2,1,0:T(8,128)(2,1)} %m_hbm.1, bf16[2,128,4096]{2,1,0:T(8,128)(2,1)} %x_hbm.1, bf16[2,512,512]{2,1,0:T(8,128)(2,1)} %og_hbm.1), custom_call_target="tpu_custom_call" | custom-call | tf_op jit(solution)/shard_map/pallas_call | solution.py:377
  270.8 0.0 copy-start
  270.8 4.6 %copy.10 = bf16[1,4096,512]{2,1,0:T(8,128)(2,1)} copy(bf16[1,4096,512]{2,1,0:T(8,128)(2,1)} %get-tuple-element.6) | data formatting | bytes 8388608
  275.4 0.0 copy-done
  275.4 0.0 copy-start.1
  275.4 2.1 copy.11
  277.5 1.0 copy-done.1
  278.5 1.3 copy.12
Async XLA Ops:
  270.8 4.6 %copy-start = (bf16[1,4096,512]{2,1,0:T(8,128)(2,1)S(1)}, bf16[1,4096,512]{2,1,0:T(8,128)(2,1)}, u32[]{:S(2)}) copy-start(bf16[1,4096,512]{2,1,0:T(8,128)(2,1)} %get-tuple-element.7) | copy-start | bytes 12582916
  275.4 3.1 %copy-start.1 = (bf16[2,128,4096]{2,1,0:T(8,128)(2,1)S(1)}, bf16[2,128,4096]{2,1,0:T(8,128)(2,1)}, u32[]{:S(2)}) copy-start(bf16[2,128,4096]{2,1,0:T(8,128)(2,1)} %get-tuple-element.8) | copy-start | bytes 6291460

commit v2 on v1

--- a/solution.py
+++ b/solution.py
@@ -11,11 +11,11 @@
 bf16 = jnp.bfloat16
 f32 = jnp.float32
 
-CHUNKS = 4
+CHUNKS = 8
 TRANSFERS = (
-    "x0n", "x0f", "x0c0", "x0fn", "x0nf", "x0c1", "x1n", "x1f", "x1c", "x1fn", "x1nf", "x1c1",
-    "xbc", "xca", "xcb", "xcc", "q", "s1n", "s1x", "s1c", "s1bc", "st", "p0c", "a0f", "a0n", "a0fn",
-    "a0nf", "a1n", "a1f", "to_near", "to_far",
+    "x0n0", "x0n1", "x0f0", "x0f1", "x0c0", "x0fn0", "x0fn1", "x0nf0", "x0nf1", "x0c1", "x1n",
+    "x1f", "x1c", "x1fn", "x1nf", "x1c1", "xbc", "xca", "xcb", "xcd", "xcc", "q", "s1n", "s1x",
+    "s1c", "s1bc", "st", "p0c", "a0f", "a0n", "a0fn", "a0nf", "a1n", "a1f", "to_near", "to_far",
 )
 NUMBER = {name: k for k, name in enumerate(TRANSFERS)}
 CHAINS = {name: len(TRANSFERS) + CHUNKS * k for k, name in enumerate(("w1", "w2", "w3", "m1", "m2", "m3"))}
@@ -43,9 +43,9 @@
     cut = rows // 2
     half = d // 2
     chunk = half // CHUNKS
-    tile = chunk // 2
+    piece_rows = cut // 2
+    most = rows - cut // 2
     pair = 2 * rows
-    n = 4 * rows
 
     r = lax.axis_index("replica")
     t = lax.axis_index("tensor")
@@ -59,11 +59,12 @@
     near = (r_near, t)
     far = (r_near, t_far)
     across = (r + 2 - 4 * lower, t)
+    beyond = (r, t_far)
 
     barrier = pltpu.get_barrier_semaphore()
-    for there in (core, near, far, across):
+    for there in (core, near, far, across, beyond):
         pl.semaphore_signal(barrier, inc=1, device_id=there, device_id_type=pl.DeviceIdType.MESH)
-    pl.semaphore_wait(barrier, 4)
+    pl.semaphore_wait(barrier, 5)
 
     def piece(start, size):
         return pl.ds(pl.multiple_of(start, size), size)
@@ -75,11 +76,15 @@
         )
 
     routes = {
-        "x0n": (x_hbm.at[0, pl.ds(cut, cut)], tn, near),
-        "x0f": (x_hbm.at[0, pl.ds(0, cut)], tf, far),
+        "x0n0": (x_hbm.at[0, pl.ds(cut, piece_rows)], tn.at[pl.ds(0, piece_rows)], near),
+        "x0n1": (x_hbm.at[0, pl.ds(most, piece_rows)], tn.at[pl.ds(piece_rows, piece_rows)], near),
+        "x0f0": (x_hbm.at[0, pl.ds(0, piece_rows)], tf.at[pl.ds(0, piece_rows)], far),
+        "x0f1": (x_hbm.at[0, pl.ds(piece_rows, piece_rows)], tf.at[pl.ds(piece_rows, piece_rows)], far),
         "x0c0": (x_hbm.at[0], x0.at[pl.ds(pair, rows)], core),
-        "x0fn": (tf, x0.at[pl.ds(rows, cut)], near),
-        "x0nf": (tn, x0.at[pl.ds(rows + cut, cut)], far),
+        "x0fn0": (tf.at[pl.ds(0, piece_rows)], x0.at[pl.ds(rows, piece_rows)], near),
+        "x0fn1": (tf.at[pl.ds(piece_rows, piece_rows)], x0.at[pl.ds(rows + piece_rows, piece_rows)], near),
+        "x0nf0": (tn.at[pl.ds(0, piece_rows)], x0.at[pl.ds(rows + cut, piece_rows)], far),
+        "x0nf1": (tn.at[pl.ds(piece_rows, piece_rows)], x0.at[pl.ds(rows + most, piece_rows)], far),
         "x0c1": (x0.at[pl.ds(rows, rows)], x0.at[pl.ds(pair + rows, rows)], core),
         "x1n": (x_hbm.at[1], xb.at[pl.ds(0, rows)], near),
         "x1f": (x_hbm.at[1], xb.at[pl.ds(rows, rows)], far),
@@ -89,7 +94,8 @@
         "x1c1": (xa.at[pl.ds(rows, rows)], xa.at[pl.ds(pair + rows, rows)], core),
         "xbc": (xb.at[pl.ds(0, pair)], xb.at[pl.ds(pair, pair)], core),
         "xca": (x_hbm.at[1], xc.at[pl.ds(0, rows)], across),
-        "xcb": (xa.at[pl.ds(rows, rows)], xc.at[pl.ds(rows, rows)], across),
+        "xcb": (xa.at[pl.ds(rows, most)], xc.at[pl.ds(rows, most)], across),
+        "xcd": (xc.at[pl.ds(most, piece_rows)], xc.at[pl.ds(rows + most, piece_rows)], beyond),
         "xcc": (xc.at[pl.ds(0, pair)], xc.at[pl.ds(pair, pair)], core),
         "q": (q_give, q_got, near),
         "s1n": (s1, s1b, near),
@@ -153,77 +159,17 @@
             body(i)
 
     loads[0].start()
-    go("x0f", "x0n", "x0c0")
-    loads[1].start()
-    loads[2].start()
+    go("x0f0", "x0n0", "x0f1", "x0n1", "x0c0")
     each(CHUNKS, lambda i: link("w1", i).start())
-    loads[4].start()
-    loads[3].start()
-    arrived("x0f")
-    go("x0fn")
-    arrived("x0n")
-    go("x0nf", "x1n", "x1f", "x1c")
-    arrived("x0fn", "x0nf")
-    go("x0c1")
-    loads[0].wait()
+    for load_now in loads[1:]:
+        load_now.start()
+    for k in "01":
+        arrived("x0f" + k)
+        go("x0fn" + k)
+        arrived("x0n" + k)
+        go("x0nf" + k)
+    go("x1n", "x1f", "x1c")
     loads[1].wait()
-    loads[2].wait()
-    arrived("x0c0", "x0c1")
-
-    depth = d // 8
-
-    def product(out, lhs, rhs):
-        out[...] = jnp.zeros_like(out)
-
-        def add(k):
-            here = piece(k * depth, depth)
-            out[...] += dot(lhs[:, here], rhs[here, :], 1, 0)
-
-        each(d // depth, add)
-
-    def slopes(out, step, pre):
-        for j, block in enumerate((t, t_far, t_core, (t_core + 2) % 4)):
-            up = og[step, piece(block * rows, rows), :].astype(f32)
-            here = pl.ds(j * rows, rows)
-            out[here, :] = (up * silu_slope(pre(here))).astype(bf16)
-
-    product(q_own, x0, wv)
-    slopes(s0, 0, lambda here: q_own[here, :])
-    loads[4].wait()
-
-    def moment_tile(start):
-        here = piece(start, tile)
-        grad = dot(x0[:, here], s0[...], 0, 0)
-        moment = (mom_decay * mv[here, :].astype(f32) + grad).astype(bf16)
-        mv[here, :] = moment
-        stepped[here, :] = (wv[here, :].astype(f32) - learn_rate * moment.astype(f32)).astype(bf16)
-
-    def moment_chunk(i):
-        moment_tile(give0 + i * chunk)
-        moment_tile(give0 + i * chunk + tile)
-        link("m1", i).start()
-
-    each(CHUNKS, moment_chunk)
-    each(half // tile, lambda i: moment_tile(keep0 + i * tile))
-    go("st")
-
-    arrived("x1f")
-    go("x1fn")
-    arrived("x1n")
-    go("x1nf")
-
-    sent("x0c1")
-
-    def part0(first):
-        def one(k):
-            here = piece(k * tile, tile)
-            x0[pl.ds(first, pair), here] = dot(s0[pl.ds(first, pair), :], wv[here, :], 1, 1).astype(bf16)
-
-        each(d // tile, one)
-
-    part0(pair)
-    go("p0c")
-    part0(0)
 
     def pair_chunk(own, landed, first, second, i):
         link(first, i).wait_recv()
@@ -238,31 +184,85 @@
         other[here, :] = ((landed[here, :].astype(f32) + other[here, :].astype(f32)) * 0.5).astype(bf16)
         link(third, i).start()
 
-    each(CHUNKS // 2, lambda i: pair_chunk(wv, lw1, "w1", "w2", i))
-
-    loads[3].wait()
-    arrived("x1fn", "x1nf")
-    go("x1c1", "xbc")
+    pair_chunk(wv, lw1, "w1", "w2", 0)
+    loads[0].wait()
+    loads[2].wait()
+    arrived("x0c0", "x0fn0", "x0fn1", "x0nf0", "x0nf1")
+    go("x0c1")
+    arrived("x0c1")
+
+    depth = d // 8
+
+    def product(out, lhs, rhs):
+        out[...] = jnp.zeros_like(out)
+
+        def add(k):
+            here = piece(k * depth, depth)
+            out[...] += dot(lhs[:, here], rhs[here, :], 1, 0)
+
+        each(d // depth, add)
+
+    def slopes(out, step, pre):
+        for j, block in enumerate((t, t_far, t_core, (t_core + 2) % 4)):
+            up = og[step, piece(block * rows, rows), :].astype(f32)
+            here = pl.ds(j * rows, rows)
+            out[here, :] = (up * silu_slope(pre(here))).astype(bf16)
+
+    product(q_own, x0, wv)
+    slopes(s0, 0, lambda here: q_own[here, :])
+    loads[4].wait()
+
+    def moment_tile(start):
+        here = piece(start, chunk)
+        grad = dot(x0[:, here], s0[...], 0, 0)
+        moment = (mom_decay * mv[here, :].astype(f32) + grad).astype(bf16)
+        mv[here, :] = moment
+        stepped[here, :] = (wv[here, :].astype(f32) - learn_rate * moment.astype(f32)).astype(bf16)
+
+    def moment_chunk(i):
+        moment_tile(give0 + i * chunk)
+        link("m1", i).start()
+
+    each(CHUNKS, moment_chunk)
+    each(CHUNKS, lambda i: moment_tile(keep0 + i * chunk))
+    go("st", "xca")
+
+    sent("x0c1")
+
+    def part0(first):
+        def one(k):
+            here = piece(k * chunk, chunk)
+            x0[pl.ds(first, pair), here] = dot(s0[pl.ds(first, pair), :], wv[here, :], 1, 1).astype(bf16)
+
+        each(d // chunk, one)
+
+    part0(pair)
+    go("p0c")
+    part0(0)
+
+    arrived("x1f")
+    go("x1fn")
+    arrived("x1n")
+    go("x1nf", "xbc")
     arrived("p0c")
     lp0[pl.ds(rows, rows), :] = (
         x0[pl.ds(rows, rows), :].astype(f32) + lp0[pl.ds(rows, rows), :].astype(f32)
     ).astype(bf16)
-    go("a0f", "a0n")
-
-    arrived("x1c", "x1c1", "xbc")
-    product(q_give, xb, stepped)
+
+    arrived("xbc")
+    product(q_own, xb, stepped)
+    q_give[...] = q_own[...].astype(bf16)
     go("q")
+    pair_chunk(wv, lw1, "w1", "w2", 1)
+    loads[3].wait()
+    arrived("x1fn", "x1nf")
+    go("x1c1", "xcb")
+    arrived("x1c", "x1c1")
     product(q_own, xa, stepped)
-    go("xca")
-    arrived("a0f")
-    go("a0fn")
-    arrived("a0n")
-    go("a0nf")
-    each(CHUNKS // 2, lambda i: pair_chunk(wv, lw1, "w1", "w2", i + CHUNKS // 2))
     arrived("q")
-    slopes(s1, 1, lambda here: (q_own[here, :] + q_got[here, :]) * 0.5)
-    go("s1c", "s1n", "s1x", "xcb")
-    each(CHUNKS, lambda i: pair_chunk(mv, lm1, "m1", "m2", i))
+    slopes(s1, 1, lambda here: (q_own[here, :] + q_got[here, :].astype(f32)) * 0.5)
+    go("s1n", "s1x", "s1c")
+    each(CHUNKS - 2, lambda i: pair_chunk(wv, lw1, "w1", "w2", i + 2))
     arrived("s1n")
     go("s1bc")
     arrived("s1c", "s1bc", "st")
@@ -270,16 +270,19 @@
     sent("x1fn", "x1nf", "xbc")
 
     def part1(k):
-        here = piece(k * tile, tile)
+        here = piece(k * chunk, chunk)
         mine = jnp.concatenate([s1[pl.ds(0, pair), :], s1b[pl.ds(0, pair), :]], axis=0)
         theirs = jnp.concatenate([s1o[...], s1bo[...]], axis=0)
         both = dot(mine, stepped[here, :], 1, 1) + dot(theirs, stepped_o[here, :], 1, 1)
         xb[:, here] = (both * 0.5).astype(bf16)
 
-    each(d // tile, part1)
+    each(d // chunk, part1)
     go("a1n", "a1f")
 
+    each(CHUNKS, lambda i: pair_chunk(mv, lm1, "m1", "m2", i))
     each(CHUNKS, lambda i: mean_chunk(lw1, lw2, "w2", "w3", i))
+    arrived("xca")
+    go("xcd", "a0n", "a0f")
     arrived("a1n")
     here = pl.ds(pair + rows, cut)
     xb[here, :] = (xb[here, :].astype(f32) + t1n[...].astype(f32)).astype(bf16)
@@ -288,9 +291,48 @@
     here = pl.ds(pair + cut, cut)
     xb[here, :] = (xb[here, :].astype(f32) + t1f[...].astype(f32)).astype(bf16)
     go("to_near")
-    arrived("xca", "xcb")
+    arrived("a0f")
+    go("a0fn")
+    each(CHUNKS, lambda i: mean_chunk(lm1, lm2, "m2", "m3", i))
+    arrived("xcb", "xcd")
     go("xcc")
-    each(CHUNKS, lambda i: mean_chunk(lm1, lm2, "m2", "m3", i))
+    arrived("a0n")
+    go("a0nf")
+
+    arrived("s1x", "xcc")
+    each(CHUNKS, lambda i: link("m1", i).wait_send())
+
+    def finish(w_mean, m_mean, start, i):
+        from_ = piece(i * chunk, chunk)
+        here = piece(start + i * chunk, chunk)
+        grad = dot(xa[:, here], s1[...], 0, 0) + dot(xc[:, here], s1c[...], 0, 0)
+        m_now = m_mean[from_, :].astype(f32)
+        moment = (mom_decay * m_now + grad * 0.5).astype(bf16)
+        mv[here, :] = moment
+        wv[here, :] = (
+            w_mean[from_, :].astype(f32) - learn_rate * (m_now + moment.astype(f32))
+        ).astype(bf16)
+
+    each(CHUNKS, lambda i: finish(lw2, lm2, keep0, i))
+    load(1, wv.at[piece(keep0, half)], new_w.at[0, piece(keep0, half)]).start()
+    load(2, mv.at[piece(keep0, half)], new_m.at[0, piece(keep0, half)]).start()
+
+    def last_w(i):
+        there = piece(give0 + i * chunk, chunk)
+        return load(5 + i, wv.at[there], new_w.at[0, there])
+
+    def last_m(i):
+        there = piece(give0 + i * chunk, chunk)
+        return load(5 + CHUNKS + i, mv.at[there], new_m.at[0, there])
+
+    def finish_chunk(i):
+        link("w3", i).wait_recv()
+        link("m3", i).wait_recv()
+        finish(lw3, lm3, give0, i)
+        last_w(i).start()
+        last_m(i).start()
+
+    each(CHUNKS - 1, finish_chunk)
 
     arrived("a0fn", "a0nf")
     for k, back in enumerate((r0n, r0f)):
@@ -299,47 +341,11 @@
             x0[here, :].astype(f32) + lp0[here, :].astype(f32) + back[...].astype(f32)
         ).astype(bf16)
     load(0, x0.at[pl.ds(0, rows)], grad_in.at[0]).start()
-
-    arrived("s1x", "xcc")
-    each(CHUNKS, lambda i: link("m1", i).wait_send())
-
-    def finish(w_mean, m_mean, start, i):
-        from_ = piece(i * tile, tile)
-        here = piece(start + i * tile, tile)
-        grad = dot(xa[:, here], s1[...], 0, 0) + dot(xc[:, here], s1c[...], 0, 0)
-        m_now = m_mean[from_, :].astype(f32)
-        moment = (mom_decay * m_now + grad * 0.5).astype(bf16)
-        mv[here, :] = moment
-        wv[here, :] = (
-            w_mean[from_, :].astype(f32) - learn_rate * (m_now + moment.astype(f32))
-        ).astype(bf16)
-
-    each(half // tile, lambda i: finish(lw2, lm2, keep0, i))
-    load(1, wv.at[piece(keep0, half)], new_w.at[0, piece(keep0, half)]).start()
-    load(2, mv.at[piece(keep0, half)], new_m.at[0, piece(keep0, half)]).start()
-
     arrived("to_near", "to_far")
     x_first = xb[pl.ds(0, rows), :].astype(f32)
     xb[pl.ds(0, rows), :] = (x_first + r1n[...].astype(f32) + r1f[...].astype(f32)).astype(bf16)
     load(3, xb.at[pl.ds(0, rows)], grad_in.at[1]).start()
-
-    def last_w(i):
-        there = piece(give0 + i * chunk, chunk)
-        return load(5 + i, wv.at[there], new_w.at[0, there])
-
-    def last_m(i):
-        there = piece(give0 + i * chunk, chunk)
-        return load(5 + CHUNKS + i, mv.at[there], new_m.at[0, there])
-
-    def finish_chunk(i):
-        link("w3", i).wait_recv()
-        link("m3", i).wait_recv()
-        finish(lw3, lm3, give0, 2 * i)
-        finish(lw3, lm3, give0, 2 * i + 1)
-        last_w(i).start()
-        last_m(i).start()
-
-    each(CHUNKS, finish_chunk)
+    finish_chunk(CHUNKS - 1)
 
     sent(*[name for name in TRANSFERS if name not in ("x0c1", "x1fn", "x1nf", "xbc")])
 
@@ -369,7 +375,8 @@
         + [((pair, d), bf16)]
         + [((cut, d), bf16)] * 6
         + [((rows, d), bf16)] * 2
-        + [((n, cols), f32)] * 3
+        + [((n, cols), f32)]
+        + [((n, cols), bf16)] * 2
         + [((2, n, cols), bf16)]
         + [((n, cols), bf16)] * 4
         + [((pair, cols), bf16)] * 2

time: 280 us -> 250 us (0.89)
  Pallas kernels: 270 us -> 240 us
    pallas_call x1, Pallas kernels: 270 us -> 240 us  [local(): pl.pallas_call(kernel, out_shape=(jax.ShapeDtypeStruct(weight.shape, bf16...]
where the time goes in v2:
time: 250 us
  Pallas kernels  240 us (96%)
  local copies, waits for them, and re-layouts  9.06 us (4%)
    pallas_call x1, Pallas kernels, local(): pl.pallas_call(kernel, out_shape=(jax.ShapeDtypeStruct(weight.shape, bf16...  240 us
    unnamed x7, local copies, waits for them, and re-layouts  9.06 us

profile of v2, /device:TPU:0, one launch (start us, length us, event | category | flops | bytes accessed | tf_op | source)
XLA Modules:
  0.0 249.7 jit_solution(16112671450207876978)
XLA Ops:
  0.6 240.0 %shard_map.67 = (bf16[1,4096,512]{2,1,0:T(8,128)(2,1)}, bf16[1,4096,512]{2,1,0:T(8,128)(2,1)}, bf16[2,128,4096]{2,1,0:T(8,128)(2,1)}) custom-call(bf16[1,4096,512]{2,1,0:T(8,128)(2,1)} %w_hbm.1, bf16[1,4096,512]{2,1,0:T(8,128)(2,1)} %m_hbm.1, bf16[2,128,4096]{2,1,0:T(8,128)(2,1)} %x_hbm.1, bf16[2,512,512]{2,1,0:T(8,128)(2,1)} %og_hbm.1), custom_call_target="tpu_custom_call" | custom-call | tf_op jit(solution)/shard_map/pallas_call | solution.py:384
  240.6 0.0 copy-start
  240.6 4.6 %copy.10 = bf16[1,4096,512]{2,1,0:T(8,128)(2,1)} copy(bf16[1,4096,512]{2,1,0:T(8,128)(2,1)} %get-tuple-element.6) | data formatting | bytes 8388608
  245.2 0.0 copy-done
  245.2 0.0 copy-start.1
  245.2 2.1 copy.11
  247.4 1.0 copy-done.1
  248.3 1.3 copy.12
Async XLA Ops:
  240.6 4.6 %copy-start = (bf16[1,4096,512]{2,1,0:T(8,128)(2,1)S(1)}, bf16[1,4096,512]{2,1,0:T(8,128)(2,1)}, u32[]{:S(2)}) copy-start(bf16[1,4096,512]{2,1,0:T(8,128)(2,1)} %get-tuple-element.7) | copy-start | bytes 12582916
  245.2 3.1 %copy-start.1 = (bf16[2,128,4096]{2,1,0:T(8,128)(2,1)S(1)}, bf16[2,128,4096]{2,1,0:T(8,128)(2,1)}, u32[]{:S(2)}) copy-start(bf16[2,128,4096]{2,1,0:T(8,128)(2,1)} %get-tuple-element.8) | copy-start | bytes 6291460

commit v3 on v2

--- a/solution.py
+++ b/solution.py
@@ -13,9 +13,9 @@
 
 CHUNKS = 8
 TRANSFERS = (
-    "x0n0", "x0n1", "x0f0", "x0f1", "x0c0", "x0fn0", "x0fn1", "x0nf0", "x0nf1", "x0c1", "x1n",
-    "x1f", "x1c", "x1fn", "x1nf", "x1c1", "xbc", "xca", "xcb", "xcd", "xcc", "q", "s1n", "s1x",
-    "s1c", "s1bc", "st", "p0c", "a0f", "a0n", "a0fn", "a0nf", "a1n", "a1f", "to_near", "to_far",
+    "x0n0", "x0n1", "x0f0", "x0f1", "x0c0", "x0fn0", "x0fn1", "x0nf0", "x0nf1", "x0c1", "x1n0",
+    "x1n1", "x1f", "x1c", "x1nf0", "x1nf1", "x1c1", "xbc", "xca", "xcb", "xcd", "xcc", "q", "s1n",
+    "s1x", "s1c", "s1bc", "st", "p0c", "a0f", "a0n", "a0fn", "a0nf", "a1f", "to_near", "to_far",
 )
 NUMBER = {name: k for k, name in enumerate(TRANSFERS)}
 CHAINS = {name: len(TRANSFERS) + CHUNKS * k for k, name in enumerate(("w1", "w2", "w3", "m1", "m2", "m3"))}
@@ -34,7 +34,7 @@
 def kernel(
     w_hbm, m_hbm, x_hbm, og_hbm, new_w, new_m, grad_in,
     wv, mv, stepped, stepped_o, x0, xa, xb, xc, lw1, lw2, lw3, lm1, lm2, lm3,
-    tn, tf, lp0, t0n, t0f, r0n, r0f, t1n, t1f, r1n, r1f,
+    tn, tf, lp0, t0n, t0f, r0n, r0f, t1f, r1n, r1f,
     q_own, q_give, q_got, og, s0, s1, s1b, s1c, s1o, s1bo,
     send, recv, local,
 ):
@@ -86,16 +86,17 @@
         "x0nf0": (tn.at[pl.ds(0, piece_rows)], x0.at[pl.ds(rows + cut, piece_rows)], far),
         "x0nf1": (tn.at[pl.ds(piece_rows, piece_rows)], x0.at[pl.ds(rows + most, piece_rows)], far),
         "x0c1": (x0.at[pl.ds(rows, rows)], x0.at[pl.ds(pair + rows, rows)], core),
-        "x1n": (x_hbm.at[1], xb.at[pl.ds(0, rows)], near),
+        "x1n0": (x_hbm.at[1, pl.ds(0, cut)], xb.at[pl.ds(0, cut)], near),
+        "x1n1": (x_hbm.at[1, pl.ds(cut, cut)], xb.at[pl.ds(cut, cut)], near),
         "x1f": (x_hbm.at[1], xb.at[pl.ds(rows, rows)], far),
         "x1c": (x_hbm.at[1], xa.at[pl.ds(pair, rows)], core),
-        "x1fn": (xb.at[pl.ds(rows, cut)], xa.at[pl.ds(rows, cut)], near),
-        "x1nf": (xb.at[pl.ds(cut, cut)], xa.at[pl.ds(rows + cut, cut)], far),
+        "x1nf0": (xb.at[pl.ds(0, cut)], xa.at[pl.ds(rows, cut)], far),
+        "x1nf1": (xb.at[pl.ds(cut, cut)], xa.at[pl.ds(rows + cut, cut)], far),
         "x1c1": (xa.at[pl.ds(rows, rows)], xa.at[pl.ds(pair + rows, rows)], core),
         "xbc": (xb.at[pl.ds(0, pair)], xb.at[pl.ds(pair, pair)], core),
         "xca": (x_hbm.at[1], xc.at[pl.ds(0, rows)], across),
-        "xcb": (xa.at[pl.ds(rows, most)], xc.at[pl.ds(rows, most)], across),
-        "xcd": (xc.at[pl.ds(most, piece_rows)], xc.at[pl.ds(rows + most, piece_rows)], beyond),
+        "xcb": (xa.at[pl.ds(rows, piece_rows)], xc.at[pl.ds(rows, piece_rows)], across),
+        "xcd": (xc.at[pl.ds(piece_rows, most)], xc.at[pl.ds(rows + piece_rows, most)], beyond),
         "xcc": (xc.at[pl.ds(0, pair)], xc.at[pl.ds(pair, pair)], core),
         "q": (q_give, q_got, near),
         "s1n": (s1, s1b, near),
@@ -108,8 +109,7 @@
         "a0n": (lp0.at[pl.ds(rows + cut, cut)], t0n, near),
         "a0fn": (t0f, r0n, near),
         "a0nf": (t0n, r0f, far),
-        "a1n": (xb.at[pl.ds(rows, cut)], t1n, near),
-        "a1f": (xb.at[pl.ds(rows + cut, cut)], t1f, far),
+        "a1f": (xb.at[pl.ds(rows, rows)], t1f, far),
         "to_near": (xb.at[pl.ds(pair, rows)], r1n, near),
         "to_far": (xb.at[pl.ds(pair + rows, rows)], r1f, far),
     }
@@ -168,7 +168,7 @@
         go("x0fn" + k)
         arrived("x0n" + k)
         go("x0nf" + k)
-    go("x1n", "x1f", "x1c")
+    go("x1n0", "x1n1", "x1f", "x1c")
     loads[1].wait()
 
     def pair_chunk(own, landed, first, second, i):
@@ -184,7 +184,7 @@
         other[here, :] = ((landed[here, :].astype(f32) + other[here, :].astype(f32)) * 0.5).astype(bf16)
         link(third, i).start()
 
-    pair_chunk(wv, lw1, "w1", "w2", 0)
+    each(2, lambda i: pair_chunk(wv, lw1, "w1", "w2", i))
     loads[0].wait()
     loads[2].wait()
     arrived("x0c0", "x0fn0", "x0fn1", "x0nf0", "x0nf1")
@@ -228,6 +228,8 @@
     go("st", "xca")
 
     sent("x0c1")
+    arrived("x1n0")
+    go("x1nf0")
 
     def part0(first):
         def one(k):
@@ -240,10 +242,10 @@
     go("p0c")
     part0(0)
 
+    arrived("x1n1")
+    go("x1nf1")
     arrived("x1f")
-    go("x1fn")
-    arrived("x1n")
-    go("x1nf", "xbc")
+    go("xbc")
     arrived("p0c")
     lp0[pl.ds(rows, rows), :] = (
         x0[pl.ds(rows, rows), :].astype(f32) + lp0[pl.ds(rows, rows), :].astype(f32)
@@ -253,21 +255,21 @@
     product(q_own, xb, stepped)
     q_give[...] = q_own[...].astype(bf16)
     go("q")
-    pair_chunk(wv, lw1, "w1", "w2", 1)
+    each(2, lambda i: pair_chunk(wv, lw1, "w1", "w2", i + 2))
     loads[3].wait()
-    arrived("x1fn", "x1nf")
+    arrived("x1nf0", "x1nf1")
     go("x1c1", "xcb")
     arrived("x1c", "x1c1")
     product(q_own, xa, stepped)
     arrived("q")
     slopes(s1, 1, lambda here: (q_own[here, :] + q_got[here, :].astype(f32)) * 0.5)
     go("s1n", "s1x", "s1c")
-    each(CHUNKS - 2, lambda i: pair_chunk(wv, lw1, "w1", "w2", i + 2))
+    each(CHUNKS - 4, lambda i: pair_chunk(wv, lw1, "w1", "w2", i + 4))
     arrived("s1n")
     go("s1bc")
     arrived("s1c", "s1bc", "st")
 
-    sent("x1fn", "x1nf", "xbc")
+    sent("x1nf0", "x1nf1", "xbc")
 
     def part1(k):
         here = piece(k * chunk, chunk)
@@ -277,18 +279,14 @@
         xb[:, here] = (both * 0.5).astype(bf16)
 
     each(d // chunk, part1)
-    go("a1n", "a1f")
+    go("a1f", "to_far")
 
     each(CHUNKS, lambda i: pair_chunk(mv, lm1, "m1", "m2", i))
     each(CHUNKS, lambda i: mean_chunk(lw1, lw2, "w2", "w3", i))
     arrived("xca")
     go("xcd", "a0n", "a0f")
-    arrived("a1n")
-    here = pl.ds(pair + rows, cut)
-    xb[here, :] = (xb[here, :].astype(f32) + t1n[...].astype(f32)).astype(bf16)
-    go("to_far")
     arrived("a1f")
-    here = pl.ds(pair + cut, cut)
+    here = pl.ds(pair, rows)
     xb[here, :] = (xb[here, :].astype(f32) + t1f[...].astype(f32)).astype(bf16)
     go("to_near")
     arrived("a0f")
@@ -347,7 +345,7 @@
     load(3, xb.at[pl.ds(0, rows)], grad_in.at[1]).start()
     finish_chunk(CHUNKS - 1)
 
-    sent(*[name for name in TRANSFERS if name not in ("x0c1", "x1fn", "x1nf", "xbc")])
+    sent(*[name for name in TRANSFERS if name not in ("x0c1", "x1nf0", "x1nf1", "xbc")])
 
     def drain(i):
         for name in ("w1", "w2", "w3", "m2", "m3"):
@@ -373,8 +371,8 @@
         + [((half, cols), bf16)] * 6
         + [((cut, d), bf16)] * 2
         + [((pair, d), bf16)]
-        + [((cut, d), bf16)] * 6
-        + [((rows, d), bf16)] * 2
+        + [((cut, d), bf16)] * 4
+        + [((rows, d), bf16)] * 3
         + [((n, cols), f32)]
         + [((n, cols), bf16)] * 2
         + [((2, n, cols), bf16)]

time: 250 us -> 239 us (0.956)
  Pallas kernels: 240 us -> 229 us
    pallas_call x1, Pallas kernels: 240 us -> 229 us  [local(): pl.pallas_call(kernel, out_shape=(jax.ShapeDtypeStruct(weight.shape, bf16...]
where the time goes in v3:
time: 239 us; the launch traced here: 238 us
  Pallas kernels  229 us (96%)
  local copies, waits for them, and re-layouts  9.06 us (4%)
    pallas_call x1, Pallas kernels, local(): pl.pallas_call(kernel, out_shape=(jax.ShapeDtypeStruct(weight.shape, bf16...  229 us
    unnamed x7, local copies, waits for them, and re-layouts  9.06 us

profile of v3, /device:TPU:0, one launch (start us, length us, event | category | flops | bytes accessed | tf_op | source)
XLA Modules:
  0.0 238.4 jit_solution(6176797719688001845)
XLA Ops:
  0.6 228.7 %shard_map.67 = (bf16[1,4096,512]{2,1,0:T(8,128)(2,1)}, bf16[1,4096,512]{2,1,0:T(8,128)(2,1)}, bf16[2,128,4096]{2,1,0:T(8,128)(2,1)}) custom-call(bf16[1,4096,512]{2,1,0:T(8,128)(2,1)} %w_hbm.1, bf16[1,4096,512]{2,1,0:T(8,128)(2,1)} %m_hbm.1, bf16[2,128,4096]{2,1,0:T(8,128)(2,1)} %x_hbm.1, bf16[2,512,512]{2,1,0:T(8,128)(2,1)} %og_hbm.1), custom_call_target="tpu_custom_call" | custom-call | tf_op jit(solution)/shard_map/pallas_call | solution.py:382
  229.4 0.0 copy-start
  229.4 4.6 %copy.10 = bf16[1,4096,512]{2,1,0:T(8,128)(2,1)} copy(bf16[1,4096,512]{2,1,0:T(8,128)(2,1)} %get-tuple-element.6) | data formatting | bytes 8388608
  234.0 0.0 copy-done
  234.0 0.0 copy-start.1
  234.0 2.1 copy.11
  236.1 1.0 copy-done.1
  237.1 1.3 copy.12
Async XLA Ops:
  229.4 4.6 %copy-start = (bf16[1,4096,512]{2,1,0:T(8,128)(2,1)S(1)}, bf16[1,4096,512]{2,1,0:T(8,128)(2,1)}, u32[]{:S(2)}) copy-start(bf16[1,4096,512]{2,1,0:T(8,128)(2,1)} %get-tuple-element.7) | copy-start | bytes 12582916
  234.0 3.1 %copy-start.1 = (bf16[2,128,4096]{2,1,0:T(8,128)(2,1)S(1)}, bf16[2,128,4096]{2,1,0:T(8,128)(2,1)}, u32[]{:S(2)}) copy-start(bf16[2,128,4096]{2,1,0:T(8,128)(2,1)} %get-tuple-element.8) | copy-start | bytes 6291460

commit v4 on v3

--- a/solution.py
+++ b/solution.py
@@ -18,6 +18,7 @@
     "s1x", "s1c", "s1bc", "st", "p0c", "a0f", "a0n", "a0fn", "a0nf", "a1f", "to_near", "to_far",
 )
 NUMBER = {name: k for k, name in enumerate(TRANSFERS)}
+AWAITED = ("x0c1", "x1nf0", "x1nf1", "xbc", "x0fn0", "x0fn1", "x0nf0", "x0nf1", "p0c")
 CHAINS = {name: len(TRANSFERS) + CHUNKS * k for k, name in enumerate(("w1", "w2", "w3", "m1", "m2", "m3"))}
 COPIES = len(TRANSFERS) + CHUNKS * len(CHAINS)
 
@@ -33,12 +34,12 @@
 
 def kernel(
     w_hbm, m_hbm, x_hbm, og_hbm, new_w, new_m, grad_in,
-    wv, mv, stepped, stepped_o, x0, xa, xb, xc, lw1, lw2, lw3, lm1, lm2, lm3,
-    tn, tf, lp0, t0n, t0f, r0n, r0f, t1f, r1n, r1f,
-    q_own, q_give, q_got, og, s0, s1, s1b, s1c, s1o, s1bo,
+    stepped, stepped_o, x0, xa, xb, xc, lw1, lw2, lw3, lm1, lm2, lm3,
+    tn, tf, lp0, t1f, r1f, q_own, q_got, og, s0, s1b, s1c, s1o, s1bo,
     send, recv, local,
 ):
-    d, cols = wv.shape
+    wv, mv = new_w.at[0], new_m.at[0]
+    d, cols = stepped.shape
     rows = x0.shape[0] // 4
     cut = rows // 2
     half = d // 2
@@ -46,6 +47,12 @@
     piece_rows = cut // 2
     most = rows - cut // 2
     pair = 2 * rows
+    s1 = s0
+    q_give = og.at[0]
+    t0n, t0f = tn, tf
+    r1n = x0.at[pl.ds(pair, rows)]
+    r0n = x0.at[pl.ds(pair + rows, cut)]
+    r0f = x0.at[pl.ds(pair + rows + cut, cut)]
 
     r = lax.axis_index("replica")
     t = lax.axis_index("tensor")
@@ -243,6 +250,7 @@
     part0(0)
 
     arrived("x1n1")
+    sent("x0fn0", "x0fn1", "x0nf0", "x0nf1")
     go("x1nf1")
     arrived("x1f")
     go("xbc")
@@ -262,6 +270,7 @@
     arrived("x1c", "x1c1")
     product(q_own, xa, stepped)
     arrived("q")
+    sent("p0c")
     slopes(s1, 1, lambda here: (q_own[here, :] + q_got[here, :].astype(f32)) * 0.5)
     go("s1n", "s1x", "s1c")
     each(CHUNKS - 4, lambda i: pair_chunk(wv, lw1, "w1", "w2", i + 4))
@@ -300,9 +309,12 @@
     arrived("s1x", "xcc")
     each(CHUNKS, lambda i: link("m1", i).wait_send())
 
-    def finish(w_mean, m_mean, start, i):
+    def finish(w_mean, m_mean, start, i, wait):
         from_ = piece(i * chunk, chunk)
         here = piece(start + i * chunk, chunk)
+        if wait:
+            link("w3", i).wait_recv()
+            link("m3", i).wait_recv()
         grad = dot(xa[:, here], s1[...], 0, 0) + dot(xc[:, here], s1c[...], 0, 0)
         m_now = m_mean[from_, :].astype(f32)
         moment = (mom_decay * m_now + grad * 0.5).astype(bf16)
@@ -311,53 +323,31 @@
             w_mean[from_, :].astype(f32) - learn_rate * (m_now + moment.astype(f32))
         ).astype(bf16)
 
-    each(CHUNKS, lambda i: finish(lw2, lm2, keep0, i))
-    load(1, wv.at[piece(keep0, half)], new_w.at[0, piece(keep0, half)]).start()
-    load(2, mv.at[piece(keep0, half)], new_m.at[0, piece(keep0, half)]).start()
-
-    def last_w(i):
-        there = piece(give0 + i * chunk, chunk)
-        return load(5 + i, wv.at[there], new_w.at[0, there])
-
-    def last_m(i):
-        there = piece(give0 + i * chunk, chunk)
-        return load(5 + CHUNKS + i, mv.at[there], new_m.at[0, there])
+    each(CHUNKS, lambda i: finish(lw2, lm2, keep0, i, False))
 
     def finish_chunk(i):
-        link("w3", i).wait_recv()
-        link("m3", i).wait_recv()
-        finish(lw3, lm3, give0, i)
-        last_w(i).start()
-        last_m(i).start()
+        finish(lw3, lm3, give0, i, True)
 
     each(CHUNKS - 1, finish_chunk)
 
     arrived("a0fn", "a0nf")
     for k, back in enumerate((r0n, r0f)):
         here = pl.ds(k * cut, cut)
-        x0[here, :] = (
+        grad_in[0, here, :] = (
             x0[here, :].astype(f32) + lp0[here, :].astype(f32) + back[...].astype(f32)
         ).astype(bf16)
-    load(0, x0.at[pl.ds(0, rows)], grad_in.at[0]).start()
     arrived("to_near", "to_far")
     x_first = xb[pl.ds(0, rows), :].astype(f32)
-    xb[pl.ds(0, rows), :] = (x_first + r1n[...].astype(f32) + r1f[...].astype(f32)).astype(bf16)
-    load(3, xb.at[pl.ds(0, rows)], grad_in.at[1]).start()
+    grad_in[1, :, :] = (x_first + r1n[...].astype(f32) + r1f[...].astype(f32)).astype(bf16)
     finish_chunk(CHUNKS - 1)
 
-    sent(*[name for name in TRANSFERS if name not in ("x0c1", "x1nf0", "x1nf1", "xbc")])
+    sent(*[name for name in TRANSFERS if name not in AWAITED])
 
     def drain(i):
         for name in ("w1", "w2", "w3", "m2", "m3"):
             link(name, i).wait_send()
-        last_w(i).wait()
-        last_m(i).wait()
 
     each(CHUNKS, drain)
-    load(0, x0.at[pl.ds(0, rows)], grad_in.at[0]).wait()
-    load(1, wv.at[piece(keep0, half)], new_w.at[0, piece(keep0, half)]).wait()
-    load(2, mv.at[piece(keep0, half)], new_m.at[0, piece(keep0, half)]).wait()
-    load(3, xb.at[pl.ds(0, rows)], grad_in.at[1]).wait()
 
 
 def local(weight, momentum, inputs, out_grads):
@@ -366,36 +356,35 @@
     n, pair, cut, half = 4 * rows, 2 * rows, rows // 2, d // 2
     full = (d, cols)
     vmem = (
-        [(full, bf16)] * 4
+        [(full, bf16)] * 2
         + [((n, d), bf16)] * 4
         + [((half, cols), bf16)] * 6
         + [((cut, d), bf16)] * 2
         + [((pair, d), bf16)]
-        + [((cut, d), bf16)] * 4
-        + [((rows, d), bf16)] * 3
+        + [((rows, d), bf16)] * 2
         + [((n, cols), f32)]
-        + [((n, cols), bf16)] * 2
+        + [((n, cols), bf16)]
         + [((2, n, cols), bf16)]
-        + [((n, cols), bf16)] * 4
+        + [((n, cols), bf16)] * 3
         + [((pair, cols), bf16)] * 2
     )
     return pl.pallas_call(
         kernel,
         out_shape=(
-            jax.ShapeDtypeStruct(weight.shape, bf16),
-            jax.ShapeDtypeStruct(momentum.shape, bf16),
-            jax.ShapeDtypeStruct(inputs.shape, bf16),
+            pltpu.VMEM(weight.shape, bf16),
+            pltpu.VMEM(momentum.shape, bf16),
+            pltpu.VMEM(inputs.shape, bf16),
         ),
         in_specs=[pl.BlockSpec(memory_space=pl.ANY)] * 4,
-        out_specs=[pl.BlockSpec(memory_space=pl.ANY)] * 3,
+        out_specs=[pl.BlockSpec(memory_space=pltpu.VMEM)] * 3,
         scratch_shapes=[pltpu.VMEM(shape, kind) for shape, kind in vmem]
         + [
             pltpu.SemaphoreType.DMA((COPIES,)),
             pltpu.SemaphoreType.DMA((COPIES,)),
-            pltpu.SemaphoreType.DMA((5 + 2 * CHUNKS,)),
+            pltpu.SemaphoreType.DMA((5,)),
         ],
         compiler_params=pltpu.CompilerParams(
-            collective_id=0, has_side_effects=True, vmem_limit_bytes=63 << 20
+            collective_id=0, has_side_effects=True, vmem_limit_bytes=53 << 20
         ),
     )(weight, momentum, inputs, out_grads)
 

time: 239 us -> 235 us (0.983)
  local copies, waits for them, and re-layouts: 9.06 us -> 5.35 us
    unnamed x7 -> x3, local copies, waits for them, and re-layouts: 9.06 us -> 5.35 us
where the time goes in v4:
time: 235 us; the launch traced here: 234 us
  Pallas kernels  228 us (97%)
  local copies, waits for them, and re-layouts  5.35 us (2%)
    pallas_call x1, Pallas kernels, local(): pl.pallas_call(kernel, out_shape=(pltpu.VMEM(weight.shape, bf16), pltpu.V...  228 us
    unnamed x3, local copies, waits for them, and re-layouts  5.35 us

profile of v4, /device:TPU:0, one launch (start us, length us, event | category | flops | bytes accessed | tf_op | source)
XLA Modules:
  0.0 233.9 jit_solution(1611149470734158232)
XLA Ops:
  0.6 227.9 %shard_map.67 = (bf16[1,4096,512]{2,1,0:T(8,128)(2,1)S(1)}, bf16[1,4096,512]{2,1,0:T(8,128)(2,1)S(1)}, bf16[2,128,4096]{2,1,0:T(8,128)(2,1)S(1)}) custom-call(bf16[1,4096,512]{2,1,0:T(8,128)(2,1)} %w_hbm.1, bf16[1,4096,512]{2,1,0:T(8,128)(2,1)} %m_hbm.1, bf16[2,128,4096]{2,1,0:T(8,128)(2,1)} %x_hbm.1, bf16[2,512,512]{2,1,0:T(8,128)(2,1)} %og_hbm.1), custom_call_target="tpu_custom_call" | custom-call | tf_op jit(solution)/shard_map/pallas_call | solution.py:371
  228.5 2.0 copy.10
  230.5 1.3 copy.12
  231.8 2.0 copy.11

commit v5 on v4

--- a/solution.py
+++ b/solution.py
@@ -191,7 +191,13 @@
         other[here, :] = ((landed[here, :].astype(f32) + other[here, :].astype(f32)) * 0.5).astype(bf16)
         link(third, i).start()
 
-    each(2, lambda i: pair_chunk(wv, lw1, "w1", "w2", i))
+    def w_pairs(first, last):
+        each(last - first, lambda i: pair_chunk(wv, lw1, "w1", "w2", i + first))
+
+    def m_pairs(first, last):
+        each(last - first, lambda i: pair_chunk(mv, lm1, "m1", "m2", i + first))
+
+    w_pairs(0, 2)
     loads[0].wait()
     loads[2].wait()
     arrived("x0c0", "x0fn0", "x0fn1", "x0nf0", "x0nf1")
@@ -259,11 +265,12 @@
         x0[pl.ds(rows, rows), :].astype(f32) + lp0[pl.ds(rows, rows), :].astype(f32)
     ).astype(bf16)
 
+    w_pairs(2, 3)
     arrived("xbc")
     product(q_own, xb, stepped)
     q_give[...] = q_own[...].astype(bf16)
     go("q")
-    each(2, lambda i: pair_chunk(wv, lw1, "w1", "w2", i + 2))
+    w_pairs(3, 6)
     loads[3].wait()
     arrived("x1nf0", "x1nf1")
     go("x1c1", "xcb")
@@ -273,7 +280,8 @@
     sent("p0c")
     slopes(s1, 1, lambda here: (q_own[here, :] + q_got[here, :].astype(f32)) * 0.5)
     go("s1n", "s1x", "s1c")
-    each(CHUNKS - 4, lambda i: pair_chunk(wv, lw1, "w1", "w2", i + 4))
+    w_pairs(6, CHUNKS)
+    m_pairs(0, CHUNKS // 2)
     arrived("s1n")
     go("s1bc")
     arrived("s1c", "s1bc", "st")
@@ -290,7 +298,7 @@
     each(d // chunk, part1)
     go("a1f", "to_far")
 
-    each(CHUNKS, lambda i: pair_chunk(mv, lm1, "m1", "m2", i))
+    m_pairs(CHUNKS // 2, CHUNKS)
     each(CHUNKS, lambda i: mean_chunk(lw1, lw2, "w2", "w3", i))
     arrived("xca")
     go("xcd", "a0n", "a0f")
@@ -298,9 +306,9 @@
     here = pl.ds(pair, rows)
     xb[here, :] = (xb[here, :].astype(f32) + t1f[...].astype(f32)).astype(bf16)
     go("to_near")
+    each(CHUNKS, lambda i: mean_chunk(lm1, lm2, "m2", "m3", i))
     arrived("a0f")
     go("a0fn")
-    each(CHUNKS, lambda i: mean_chunk(lm1, lm2, "m2", "m3", i))
     arrived("xcb", "xcd")
     go("xcc")
     arrived("a0n")
@@ -348,6 +356,17 @@
             link(name, i).wait_send()
 
     each(CHUNKS, drain)
+
+
+def write_out(w_in, m_in, g_in, w_out, m_out, g_out, done):
+    copies = [
+        pltpu.make_async_copy(src, dst, done.at[k])
+        for k, (src, dst) in enumerate(((w_in, w_out), (m_in, m_out), (g_in, g_out)))
+    ]
+    for c in copies:
+        c.start()
+    for c in copies:
+        c.wait()
 
 
 def local(weight, momentum, inputs, out_grads):
@@ -368,7 +387,7 @@
         + [((n, cols), bf16)] * 3
         + [((pair, cols), bf16)] * 2
     )
-    return pl.pallas_call(
+    results = pl.pallas_call(
         kernel,
         out_shape=(
             pltpu.VMEM(weight.shape, bf16),
@@ -387,6 +406,14 @@
             collective_id=0, has_side_effects=True, vmem_limit_bytes=53 << 20
         ),
     )(weight, momentum, inputs, out_grads)
+    return pl.pallas_call(
+        write_out,
+        out_shape=[jax.ShapeDtypeStruct(a.shape, bf16) for a in (weight, momentum, inputs)],
+        in_specs=[pl.BlockSpec(memory_space=pltpu.VMEM)] * 3,
+        out_specs=[pl.BlockSpec(memory_space=pl.ANY)] * 3,
+        scratch_shapes=[pltpu.SemaphoreType.DMA((3,))],
+        compiler_params=pltpu.CompilerParams(vmem_limit_bytes=1 << 20),
+    )(*results)
 
 
 def solution(mesh):

time: 235 us -> 233 us (level)
  local copies, waits for them, and re-layouts: 5.35 us -> 0 us
  Pallas kernels: 228 us -> 232 us
    unnamed x3 -> x0, local copies, waits for them, and re-layouts: 5.35 us -> none
    pallas_call x0 -> x1, Pallas kernels: none -> 3.99 us  [local(): pl.pallas_call(write_out, out_shape=[jax.ShapeDtypeStruct(a.shape, bf16)...]
where the time goes in v5:
time: 233 us
  Pallas kernels  232 us (100%)
    pallas_call x1, Pallas kernels, local(): pl.pallas_call(kernel, out_shape=(pltpu.VMEM(weight.shape, bf16), pltpu.V...  228 us

profile of v5, /device:TPU:0, one launch (start us, length us, event | category | flops | bytes accessed | tf_op | source)
XLA Modules:
  0.0 232.5 jit_solution(6836397335326086932)
XLA Ops:
  0.6 227.9 %shard_map.67 = (bf16[1,4096,512]{2,1,0:T(8,128)(2,1)S(1)}, bf16[1,4096,512]{2,1,0:T(8,128)(2,1)S(1)}, bf16[2,128,4096]{2,1,0:T(8,128)(2,1)S(1)}) custom-call(bf16[1,4096,512]{2,1,0:T(8,128)(2,1)} %w_hbm.1, bf16[1,4096,512]{2,1,0:T(8,128)(2,1)} %m_hbm.1, bf16[2,128,4096]{2,1,0:T(8,128)(2,1)} %x_hbm.1, bf16[2,512,512]{2,1,0:T(8,128)(2,1)} %og_hbm.1), custom_call_target="tpu_custom_call" | custom-call | tf_op jit(solution)/shard_map/pallas_call | solution.py:390
  228.5 4.0 %shard_map.68 = (bf16[1,4096,512]{2,1,0:T(8,128)(2,1)}, bf16[1,4096,512]{2,1,0:T(8,128)(2,1)}, bf16[2,128,4096]{2,1,0:T(8,128)(2,1)}) custom-call(bf16[1,4096,512]{2,1,0:T(8,128)(2,1)S(1)} %get-tuple-element.6.w_in, bf16[1,4096,512]{2,1,0:T(8,128)(2,1)S(1)} %get-tuple-element.7.m_in, bf16[2,128,4096]{2,1,0:T(8,128)(2,1)S(1)} %get-tuple-element.8.g_in), custom_call_target="tpu_custom_call" | custom-call | tf_op jit(solution)/shard_map/pallas_call | solution.py:409

commit v6 on v5

--- a/solution.py
+++ b/solution.py
@@ -317,13 +317,10 @@
     arrived("s1x", "xcc")
     each(CHUNKS, lambda i: link("m1", i).wait_send())
 
-    def finish(w_mean, m_mean, start, i, wait):
-        from_ = piece(i * chunk, chunk)
-        here = piece(start + i * chunk, chunk)
-        if wait:
-            link("w3", i).wait_recv()
-            link("m3", i).wait_recv()
-        grad = dot(xa[:, here], s1[...], 0, 0) + dot(xc[:, here], s1c[...], 0, 0)
+    def gradient(here):
+        return dot(xa[:, here], s1[...], 0, 0) + dot(xc[:, here], s1c[...], 0, 0)
+
+    def finish(w_mean, m_mean, from_, here, grad):
         m_now = m_mean[from_, :].astype(f32)
         moment = (mom_decay * m_now + grad * 0.5).astype(bf16)
         mv[here, :] = moment
@@ -331,37 +328,58 @@
             w_mean[from_, :].astype(f32) - learn_rate * (m_now + moment.astype(f32))
         ).astype(bf16)
 
-    each(CHUNKS, lambda i: finish(lw2, lm2, keep0, i, False))
+    def finish_kept(i):
+        here = piece(keep0 + i * chunk, chunk)
+        finish(lw2, lm2, piece(i * chunk, chunk), here, gradient(here))
 
     def finish_chunk(i):
-        finish(lw3, lm3, give0, i, True)
-
-    each(CHUNKS - 1, finish_chunk)
-
-    arrived("a0fn", "a0nf")
-    for k, back in enumerate((r0n, r0f)):
-        here = pl.ds(k * cut, cut)
-        grad_in[0, here, :] = (
-            x0[here, :].astype(f32) + lp0[here, :].astype(f32) + back[...].astype(f32)
-        ).astype(bf16)
+        here = piece(give0 + i * chunk, chunk)
+        link("w3", i).wait_recv()
+        link("m3", i).wait_recv()
+        finish(lw3, lm3, piece(i * chunk, chunk), here, gradient(here))
+
+    each(CHUNKS, finish_kept)
+    each(CHUNKS - 2, finish_chunk)
+
+    last = CHUNKS - 1
+    here = piece(give0 + last * chunk, chunk)
+    grad_last = q_own.at[pl.ds(0, chunk)]
+    grad_last[...] = gradient(here)
+
+    def drain(i):
+        for name in ("w1", "w2", "w3", "m2"):
+            link(name, i).wait_send()
+
+    late = ("to_near", "to_far", "a0fn", "a0nf")
+    each(CHUNKS, drain)
+    sent(*[name for name in TRANSFERS if name not in AWAITED + late])
     arrived("to_near", "to_far")
     x_first = xb[pl.ds(0, rows), :].astype(f32)
     grad_in[1, :, :] = (x_first + r1n[...].astype(f32) + r1f[...].astype(f32)).astype(bf16)
-    finish_chunk(CHUNKS - 1)
-
-    sent(*[name for name in TRANSFERS if name not in AWAITED])
-
-    def drain(i):
-        for name in ("w1", "w2", "w3", "m2", "m3"):
-            link(name, i).wait_send()
-
-    each(CHUNKS, drain)
+    finish_chunk(last - 1)
+    each(last, lambda i: link("m3", i).wait_send())
+    arrived("a0fn", "a0nf")
+    for k, back in enumerate((r0n, r0f)):
+        rows_of = pl.ds(k * cut, cut)
+        grad_in[0, rows_of, :] = (
+            x0[rows_of, :].astype(f32) + lp0[rows_of, :].astype(f32) + back[...].astype(f32)
+        ).astype(bf16)
+    sent(*late)
+    link("w3", last).wait_recv()
+    link("m3", last).wait_recv()
+    finish(lw3, lm3, piece(last * chunk, chunk), here, grad_last[...])
+    link("m3", last).wait_send()
 
 
 def write_out(w_in, m_in, g_in, w_out, m_out, g_out, done):
+    parts = 4
+    size = w_in.shape[1] // parts
+    pieces = [(g_in, g_out)]
+    for k in range(parts):
+        here = pl.ds(k * size, size)
+        pieces += [(w_in.at[0, here], w_out.at[0, here]), (m_in.at[0, here], m_out.at[0, here])]
     copies = [
-        pltpu.make_async_copy(src, dst, done.at[k])
-        for k, (src, dst) in enumerate(((w_in, w_out), (m_in, m_out), (g_in, g_out)))
+        pltpu.make_async_copy(src, dst, done.at[k]) for k, (src, dst) in enumerate(pieces)
     ]
     for c in copies:
         c.start()
@@ -411,7 +429,7 @@
         out_shape=[jax.ShapeDtypeStruct(a.shape, bf16) for a in (weight, momentum, inputs)],
         in_specs=[pl.BlockSpec(memory_space=pltpu.VMEM)] * 3,
         out_specs=[pl.BlockSpec(memory_space=pl.ANY)] * 3,
-        scratch_shapes=[pltpu.SemaphoreType.DMA((3,))],
+        scratch_shapes=[pltpu.SemaphoreType.DMA((9,))],
         compiler_params=pltpu.CompilerParams(vmem_limit_bytes=1 << 20),
     )(*results)
 

time: 233 us -> 232 us (level)
  no operation moved by 1% of the time
where the time goes in v6:
time: 232 us
  Pallas kernels  231 us (100%)
    pallas_call x1, Pallas kernels, local(): pl.pallas_call(kernel, out_shape=(pltpu.VMEM(weight.shape, bf16), pltpu.V...  227 us

profile of v6, /device:TPU:0, one launch (start us, length us, event | category | flops | bytes accessed | tf_op | source)
XLA Modules:
  0.0 231.8 jit_solution(6791382881155820451)
XLA Ops:
  0.6 227.2 %shard_map.67 = (bf16[1,4096,512]{2,1,0:T(8,128)(2,1)S(1)}, bf16[1,4096,512]{2,1,0:T(8,128)(2,1)S(1)}, bf16[2,128,4096]{2,1,0:T(8,128)(2,1)S(1)}) custom-call(bf16[1,4096,512]{2,1,0:T(8,128)(2,1)} %w_hbm.1, bf16[1,4096,512]{2,1,0:T(8,128)(2,1)} %m_hbm.1, bf16[2,128,4096]{2,1,0:T(8,128)(2,1)} %x_hbm.1, bf16[2,512,512]{2,1,0:T(8,128)(2,1)} %og_hbm.1), custom_call_target="tpu_custom_call" | custom-call | tf_op jit(solution)/shard_map/pallas_call | solution.py:408
  227.8 4.0 %shard_map.68 = (bf16[1,4096,512]{2,1,0:T(8,128)(2,1)}, bf16[1,4096,512]{2,1,0:T(8,128)(2,1)}, bf16[2,128,4096]{2,1,0:T(8,128)(2,1)}) custom-call(bf16[1,4096,512]{2,1,0:T(8,128)(2,1)S(1)} %get-tuple-element.6.w_in, bf16[1,4096,512]{2,1,0:T(8,128)(2,1)S(1)} %get-tuple-element.7.m_in, bf16[2,128,4096]{2,1,0:T(8,128)(2,1)S(1)} %get-tuple-element.8.g_in), custom_call_target="tpu_custom_call" | custom-call | tf_op jit(solution)/shard_map/pallas_call | solution.py:427

commit v7 on v6

--- a/solution.py
+++ b/solution.py
@@ -14,12 +14,15 @@
 CHUNKS = 8
 TRANSFERS = (
     "x0n0", "x0n1", "x0f0", "x0f1", "x0c0", "x0fn0", "x0fn1", "x0nf0", "x0nf1", "x0c1", "x1n0",
-    "x1n1", "x1f", "x1c", "x1nf0", "x1nf1", "x1c1", "xbc", "xca", "xcb", "xcd", "xcc", "q", "s1n",
-    "s1x", "s1c", "s1bc", "st", "p0c", "a0f", "a0n", "a0fn", "a0nf", "a1f", "to_near", "to_far",
+    "x1n1", "x1f", "x1c", "x1nf0", "x1nf1", "x1c1", "xbc", "q", "s1n", "s1c", "s1bc", "st", "p0c",
+    "a0f", "a0n", "a0fn", "a0nf", "a1f", "to_near", "to_far", "pg", "pk", "px", "pm",
 )
 NUMBER = {name: k for k, name in enumerate(TRANSFERS)}
-AWAITED = ("x0c1", "x1nf0", "x1nf1", "xbc", "x0fn0", "x0fn1", "x0nf0", "x0nf1", "p0c")
-CHAINS = {name: len(TRANSFERS) + CHUNKS * k for k, name in enumerate(("w1", "w2", "w3", "m1", "m2", "m3"))}
+AWAITED = ("x0c1", "x1nf0", "x1nf1", "xbc", "x0fn0", "x0fn1", "x0nf0", "x0nf1", "p0c", "pg", "pk")
+CHAINS = {
+    name: len(TRANSFERS) + CHUNKS * k
+    for k, name in enumerate(("w1", "w2", "w3", "m1", "m2", "m3", "g"))
+}
 COPIES = len(TRANSFERS) + CHUNKS * len(CHAINS)
 
 
@@ -34,8 +37,9 @@
 
 def kernel(
     w_hbm, m_hbm, x_hbm, og_hbm, new_w, new_m, grad_in,
-    stepped, stepped_o, x0, xa, xb, xc, lw1, lw2, lw3, lm1, lm2, lm3,
-    tn, tf, lp0, t1f, r1f, q_own, q_got, og, s0, s1b, s1c, s1o, s1bo,
+    stepped, stepped_o, x0, xa, xb, lw1, lw2, lw3, lm1, lm2, lm3,
+    tn, tf, lp0, t1f, r1f, q_own, q_got, og, s0, s1b, s1o, s1bo,
+    g_give, g_got, lpg, lpk, lpx,
     send, recv, local,
 ):
     wv, mv = new_w.at[0], new_m.at[0]
@@ -66,12 +70,16 @@
     near = (r_near, t)
     far = (r_near, t_far)
     across = (r + 2 - 4 * lower, t)
-    beyond = (r, t_far)
+    direct = CHUNKS // 2
+    block0 = direct * chunk
+    sub = (half - block0) // 2
+    mine0 = block0 + (r % 2) * sub
+    theirs0 = block0 + (1 - r % 2) * sub
 
     barrier = pltpu.get_barrier_semaphore()
-    for there in (core, near, far, across, beyond):
+    for there in (core, near, far, across):
         pl.semaphore_signal(barrier, inc=1, device_id=there, device_id_type=pl.DeviceIdType.MESH)
-    pl.semaphore_wait(barrier, 5)
+    pl.semaphore_wait(barrier, 4)
 
     def piece(start, size):
         return pl.ds(pl.multiple_of(start, size), size)
@@ -101,13 +109,8 @@
         "x1nf1": (xb.at[pl.ds(cut, cut)], xa.at[pl.ds(rows + cut, cut)], far),
         "x1c1": (xa.at[pl.ds(rows, rows)], xa.at[pl.ds(pair + rows, rows)], core),
         "xbc": (xb.at[pl.ds(0, pair)], xb.at[pl.ds(pair, pair)], core),
-        "xca": (x_hbm.at[1], xc.at[pl.ds(0, rows)], across),
-        "xcb": (xa.at[pl.ds(rows, piece_rows)], xc.at[pl.ds(rows, piece_rows)], across),
-        "xcd": (xc.at[pl.ds(piece_rows, most)], xc.at[pl.ds(rows + piece_rows, most)], beyond),
-        "xcc": (xc.at[pl.ds(0, pair)], xc.at[pl.ds(pair, pair)], core),
         "q": (q_give, q_got, near),
         "s1n": (s1, s1b, near),
-        "s1x": (s1, s1c, across),
         "s1c": (s1.at[pl.ds(pair, pair)], s1o, core),
         "s1bc": (s1b.at[pl.ds(pair, pair)], s1bo, core),
         "st": (stepped, stepped_o, core),
@@ -119,6 +122,10 @@
         "a1f": (xb.at[pl.ds(rows, rows)], t1f, far),
         "to_near": (xb.at[pl.ds(pair, rows)], r1n, near),
         "to_far": (xb.at[pl.ds(pair + rows, rows)], r1f, far),
+        "pg": (mv.at[piece(give0 + theirs0, sub)], lpg, near),
+        "pk": (mv.at[piece(keep0 + theirs0, sub)], lpk, near),
+        "px": (lpg, lpx, across),
+        "pm": (lm2.at[piece(mine0, sub)], lm2.at[piece(mine0, sub)], near),
     }
 
     def copy(name):
@@ -145,7 +152,8 @@
             "w3": (lw2.at[here], lw3.at[here], across),
             "m1": (mv.at[give], lm1.at[here], across),
             "m2": (lm1.at[here], lm2.at[here], near),
-            "m3": (lm2.at[here], lm3.at[here], across),
+            "m3": (mv.at[piece(keep0 + i * chunk, chunk)], lm3.at[here], across),
+            "g": (g_give.at[here], g_got.at[here], across),
         }[name]
         return remote(CHAINS[name] + i, src, dst, there)
 
@@ -185,11 +193,8 @@
         landed[here, :] = ((mine + landed[here, :].astype(f32)) * 0.5).astype(bf16)
         link(second, i).start()
 
-    def mean_chunk(landed, other, second, third, i):
-        link(second, i).wait_recv()
-        here = piece(i * chunk, chunk)
-        other[here, :] = ((landed[here, :].astype(f32) + other[here, :].astype(f32)) * 0.5).astype(bf16)
-        link(third, i).start()
+    def mean(out, left, right):
+        out[...] = ((left[...].astype(f32) + right[...].astype(f32)) * 0.5).astype(bf16)
 
     def w_pairs(first, last):
         each(last - first, lambda i: pair_chunk(wv, lw1, "w1", "w2", i + first))
@@ -197,7 +202,6 @@
     def m_pairs(first, last):
         each(last - first, lambda i: pair_chunk(mv, lm1, "m1", "m2", i + first))
 
-    w_pairs(0, 2)
     loads[0].wait()
     loads[2].wait()
     arrived("x0c0", "x0fn0", "x0fn1", "x0nf0", "x0nf1")
@@ -236,9 +240,12 @@
         moment_tile(give0 + i * chunk)
         link("m1", i).start()
 
-    each(CHUNKS, moment_chunk)
+    each(direct, moment_chunk)
+    each(CHUNKS - direct, lambda i: moment_tile(give0 + (i + direct) * chunk))
+    go("pg")
+    w_pairs(0, 1)
     each(CHUNKS, lambda i: moment_tile(keep0 + i * chunk))
-    go("st", "xca")
+    go("st")
 
     sent("x0c1")
     arrived("x1n0")
@@ -265,23 +272,56 @@
         x0[pl.ds(rows, rows), :].astype(f32) + lp0[pl.ds(rows, rows), :].astype(f32)
     ).astype(bf16)
 
-    w_pairs(2, 3)
     arrived("xbc")
     product(q_own, xb, stepped)
     q_give[...] = q_own[...].astype(bf16)
     go("q")
-    w_pairs(3, 6)
+    m_pairs(0, 1)
+    w_pairs(1, 2)
+    arrived("pg")
+    mean(lpg, lpg, mv.at[piece(give0 + mine0, sub)])
+    go("px")
     loads[3].wait()
     arrived("x1nf0", "x1nf1")
-    go("x1c1", "xcb")
+    go("x1c1")
     arrived("x1c", "x1c1")
     product(q_own, xa, stepped)
     arrived("q")
     sent("p0c")
     slopes(s1, 1, lambda here: (q_own[here, :] + q_got[here, :].astype(f32)) * 0.5)
-    go("s1n", "s1x", "s1c")
-    w_pairs(6, CHUNKS)
-    m_pairs(0, CHUNKS // 2)
+    go("s1n", "s1c", "pk")
+
+    def chunk_of(ref, i):
+        return ref.at[piece(i * chunk, chunk)]
+
+    def step_weights(i):
+        w_mean = chunk_of(lw2, i)
+        w_mean[...] = (
+            w_mean[...].astype(f32) - learn_rate * chunk_of(lm2, i)[...].astype(f32)
+        ).astype(bf16)
+        link("w3", i).start()
+
+    def direct_means(i):
+        link("w2", i).wait_recv()
+        mean(chunk_of(lw2, i), chunk_of(lw2, i), chunk_of(lw1, i))
+        link("m2", i).wait_recv()
+        mean(chunk_of(lm2, i), chunk_of(lm2, i), chunk_of(lm1, i))
+        step_weights(i)
+
+    def gradient(start):
+        return dot(xa[:, piece(start, chunk)], s1[...], 0, 0) * 0.5
+
+    def gradient_chunk(i):
+        g_give[piece(i * chunk, chunk), :] = gradient(give0 + i * chunk).astype(bf16)
+        link("g", i).start()
+
+    direct_means(0)
+    each(CHUNKS, gradient_chunk)
+    w_pairs(2, 3)
+    m_pairs(1, 2)
+    w_pairs(3, 4)
+    m_pairs(2, direct)
+    w_pairs(4, CHUNKS)
     arrived("s1n")
     go("s1bc")
     arrived("s1c", "s1bc", "st")
@@ -298,65 +338,70 @@
     each(d // chunk, part1)
     go("a1f", "to_far")
 
-    m_pairs(CHUNKS // 2, CHUNKS)
-    each(CHUNKS, lambda i: mean_chunk(lw1, lw2, "w2", "w3", i))
-    arrived("xca")
-    go("xcd", "a0n", "a0f")
+    each(direct - 1, lambda i: direct_means(i + 1))
+    arrived("pk", "px")
+    mean(lpk, lpk, mv.at[piece(keep0 + mine0, sub)])
+    mean(lm2.at[piece(mine0, sub)], lpk, lpx)
+    go("pm")
+    sent("pg", "pk")
+
+    def finish_kept(i):
+        link("g", i).wait_recv()
+        here = piece(keep0 + i * chunk, chunk)
+        grad = gradient(keep0 + i * chunk) + chunk_of(g_got, i)[...].astype(f32)
+        moment = (mom_decay * chunk_of(lm2, i)[...].astype(f32) + grad).astype(bf16)
+        mv[here, :] = moment
+        link("m3", i).start()
+        wv[here, :] = (
+            chunk_of(lw2, i)[...].astype(f32) - learn_rate * moment.astype(f32)
+        ).astype(bf16)
+
     arrived("a1f")
     here = pl.ds(pair, rows)
     xb[here, :] = (xb[here, :].astype(f32) + t1f[...].astype(f32)).astype(bf16)
-    go("to_near")
-    each(CHUNKS, lambda i: mean_chunk(lm1, lm2, "m2", "m3", i))
+    go("to_near", "a0n", "a0f")
+    each(direct, finish_kept)
+
+    arrived("pm")
+
+    def later_weights(i):
+        link("w2", i).wait_recv()
+        mean(chunk_of(lw2, i), chunk_of(lw2, i), chunk_of(lw1, i))
+        step_weights(i)
+
+    each(CHUNKS - direct, lambda i: later_weights(i + direct))
+    each(CHUNKS - direct, lambda i: finish_kept(i + direct))
     arrived("a0f")
     go("a0fn")
-    arrived("xcb", "xcd")
-    go("xcc")
+    each(direct, lambda i: link("m1", i).wait_send())
+
+    def finish_given(i):
+        link("w3", i).wait_recv()
+        link("m3", i).wait_recv()
+        here = piece(give0 + i * chunk, chunk)
+        moment = chunk_of(lm3, i)[...]
+        mv[here, :] = moment
+        wv[here, :] = (
+            chunk_of(lw3, i)[...].astype(f32) - learn_rate * moment.astype(f32)
+        ).astype(bf16)
+
+    each(direct, finish_given)
     arrived("a0n")
     go("a0nf")
 
-    arrived("s1x", "xcc")
-    each(CHUNKS, lambda i: link("m1", i).wait_send())
-
-    def gradient(here):
-        return dot(xa[:, here], s1[...], 0, 0) + dot(xc[:, here], s1c[...], 0, 0)
-
-    def finish(w_mean, m_mean, from_, here, grad):
-        m_now = m_mean[from_, :].astype(f32)
-        moment = (mom_decay * m_now + grad * 0.5).astype(bf16)
-        mv[here, :] = moment
-        wv[here, :] = (
-            w_mean[from_, :].astype(f32) - learn_rate * (m_now + moment.astype(f32))
-        ).astype(bf16)
-
-    def finish_kept(i):
-        here = piece(keep0 + i * chunk, chunk)
-        finish(lw2, lm2, piece(i * chunk, chunk), here, gradient(here))
-
-    def finish_chunk(i):
-        here = piece(give0 + i * chunk, chunk)
-        link("w3", i).wait_recv()
-        link("m3", i).wait_recv()
-        finish(lw3, lm3, piece(i * chunk, chunk), here, gradient(here))
-
-    each(CHUNKS, finish_kept)
-    each(CHUNKS - 2, finish_chunk)
-
-    last = CHUNKS - 1
-    here = piece(give0 + last * chunk, chunk)
-    grad_last = q_own.at[pl.ds(0, chunk)]
-    grad_last[...] = gradient(here)
-
     def drain(i):
-        for name in ("w1", "w2", "w3", "m2"):
+        for name in ("w1", "w2", "w3", "g"):
             link(name, i).wait_send()
 
     late = ("to_near", "to_far", "a0fn", "a0nf")
     each(CHUNKS, drain)
+    each(direct, lambda i: link("m2", i).wait_send())
     sent(*[name for name in TRANSFERS if name not in AWAITED + late])
     arrived("to_near", "to_far")
     x_first = xb[pl.ds(0, rows), :].astype(f32)
     grad_in[1, :, :] = (x_first + r1n[...].astype(f32) + r1f[...].astype(f32)).astype(bf16)
-    finish_chunk(last - 1)
+    last = CHUNKS - 1
+    each(last - direct, lambda i: finish_given(i + direct))
     each(last, lambda i: link("m3", i).wait_send())
     arrived("a0fn", "a0nf")
     for k, back in enumerate((r0n, r0f)):
@@ -365,9 +410,7 @@
             x0[rows_of, :].astype(f32) + lp0[rows_of, :].astype(f32) + back[...].astype(f32)
         ).astype(bf16)
     sent(*late)
-    link("w3", last).wait_recv()
-    link("m3", last).wait_recv()
-    finish(lw3, lm3, piece(last * chunk, chunk), here, grad_last[...])
+    finish_given(last)
     link("m3", last).wait_send()
 
 
@@ -394,7 +437,7 @@
     full = (d, cols)
     vmem = (
         [(full, bf16)] * 2
-        + [((n, d), bf16)] * 4
+        + [((n, d), bf16)] * 3
         + [((half, cols), bf16)] * 6
         + [((cut, d), bf16)] * 2
         + [((pair, d), bf16)]
@@ -402,8 +445,10 @@
         + [((n, cols), f32)]
         + [((n, cols), bf16)]
         + [((2, n, cols), bf16)]
-        + [((n, cols), bf16)] * 3
+        + [((n, cols), bf16)] * 2
         + [((pair, cols), bf16)] * 2
+        + [((half, cols), bf16)] * 2
+        + [((half // 4, cols), bf16)] * 3
     )
     results = pl.pallas_call(
         kernel,

time: 232 us -> 227 us (0.978)
  Pallas kernels: 231 us -> 226 us
    pallas_call x1, Pallas kernels: 227 us -> 222 us  [local(): pl.pallas_call(kernel, out_shape=(pltpu.VMEM(weight.shape, bf16), pltpu.V...]
where the time goes in v7:
time: 227 us
  Pallas kernels  226 us (100%)
    pallas_call x1, Pallas kernels, local(): pl.pallas_call(kernel, out_shape=(pltpu.VMEM(weight.shape, bf16), pltpu.V...  222 us

profile of v7, /device:TPU:0, one launch (start us, length us, event | category | flops | bytes accessed | tf_op | source)
XLA Modules:
  0.0 227.0 jit_solution(206795548044538771)
XLA Ops:
  0.6 222.3 %shard_map.67 = (bf16[1,4096,512]{2,1,0:T(8,128)(2,1)S(1)}, bf16[1,4096,512]{2,1,0:T(8,128)(2,1)S(1)}, bf16[2,128,4096]{2,1,0:T(8,128)(2,1)S(1)}) custom-call(bf16[1,4096,512]{2,1,0:T(8,128)(2,1)} %w_hbm.1, bf16[1,4096,512]{2,1,0:T(8,128)(2,1)} %m_hbm.1, bf16[2,128,4096]{2,1,0:T(8,128)(2,1)} %x_hbm.1, bf16[2,512,512]{2,1,0:T(8,128)(2,1)} %og_hbm.1), custom_call_target="tpu_custom_call" | custom-call | tf_op jit(solution)/shard_map/pallas_call | solution.py:453
  223.0 4.0 %shard_map.68 = (bf16[1,4096,512]{2,1,0:T(8,128)(2,1)}, bf16[1,4096,512]{2,1,0:T(8,128)(2,1)}, bf16[2,128,4096]{2,1,0:T(8,128)(2,1)}) custom-call(bf16[1,4096,512]{2,1,0:T(8,128)(2,1)S(1)} %get-tuple-element.6.w_in, bf16[1,4096,512]{2,1,0:T(8,128)(2,1)S(1)} %get-tuple-element.7.m_in, bf16[2,128,4096]{2,1,0:T(8,128)(2,1)S(1)} %get-tuple-element.8.g_in), custom_call_target="tpu_custom_call" | custom-call | tf_op jit(solution)/shard_map/pallas_call | solution.py:472

commit v8 on v7

--- a/solution.py
+++ b/solution.py
@@ -210,12 +210,16 @@
 
     depth = d // 8
 
-    def product(out, lhs, rhs):
-        out[...] = jnp.zeros_like(out)
+    def product(lhs, rhs, starts, size):
+        for first in starts:
+            q_own[pl.ds(first, size), :] = jnp.zeros((size, cols), f32)
 
         def add(k):
             here = piece(k * depth, depth)
-            out[...] += dot(lhs[:, here], rhs[here, :], 1, 0)
+            left = jnp.concatenate([lhs[pl.ds(first, size), here] for first in starts], axis=0)
+            more = dot(left, rhs[here, :], 1, 0)
+            for at, first in enumerate(starts):
+                q_own[pl.ds(first, size), :] += more[at * size : (at + 1) * size]
 
         each(d // depth, add)
 
@@ -225,7 +229,7 @@
             here = pl.ds(j * rows, rows)
             out[here, :] = (up * silu_slope(pre(here))).astype(bf16)
 
-    product(q_own, x0, wv)
+    product(x0, wv, (0,), 4 * rows)
     slopes(s0, 0, lambda here: q_own[here, :])
     loads[4].wait()
 
@@ -243,7 +247,6 @@
     each(direct, moment_chunk)
     each(CHUNKS - direct, lambda i: moment_tile(give0 + (i + direct) * chunk))
     go("pg")
-    w_pairs(0, 1)
     each(CHUNKS, lambda i: moment_tile(keep0 + i * chunk))
     go("st")
 
@@ -267,25 +270,29 @@
     go("x1nf1")
     arrived("x1f")
     go("xbc")
-    arrived("p0c")
-    lp0[pl.ds(rows, rows), :] = (
-        x0[pl.ds(rows, rows), :].astype(f32) + lp0[pl.ds(rows, rows), :].astype(f32)
-    ).astype(bf16)
-
+
+    product(xb, stepped, (0,), pair)
     arrived("xbc")
-    product(q_own, xb, stepped)
+    product(xb, stepped, (pair,), pair)
     q_give[...] = q_own[...].astype(bf16)
     go("q")
+    w_pairs(0, 1)
     m_pairs(0, 1)
     w_pairs(1, 2)
     arrived("pg")
     mean(lpg, lpg, mv.at[piece(give0 + mine0, sub)])
     go("px")
     loads[3].wait()
+    arrived("x1c")
+    product(xa, stepped, (0, pair), rows)
     arrived("x1nf0", "x1nf1")
     go("x1c1")
-    arrived("x1c", "x1c1")
-    product(q_own, xa, stepped)
+    arrived("p0c")
+    lp0[pl.ds(rows, rows), :] = (
+        x0[pl.ds(rows, rows), :].astype(f32) + lp0[pl.ds(rows, rows), :].astype(f32)
+    ).astype(bf16)
+    arrived("x1c1")
+    product(xa, stepped, (rows, pair + rows), rows)
     arrived("q")
     sent("p0c")
     slopes(s1, 1, lambda here: (q_own[here, :] + q_got[here, :].astype(f32)) * 0.5)
@@ -342,7 +349,7 @@
     arrived("pk", "px")
     mean(lpk, lpk, mv.at[piece(keep0 + mine0, sub)])
     mean(lm2.at[piece(mine0, sub)], lpk, lpx)
-    go("pm")
+    go("pm", "a0f")
     sent("pg", "pk")
 
     def finish_kept(i):
@@ -359,7 +366,7 @@
     arrived("a1f")
     here = pl.ds(pair, rows)
     xb[here, :] = (xb[here, :].astype(f32) + t1f[...].astype(f32)).astype(bf16)
-    go("to_near", "a0n", "a0f")
+    go("a0n", "to_near")
     each(direct, finish_kept)
 
     arrived("pm")

time: 227 us -> 227 us (level)
  no operation moved by 1% of the time
where the time goes in v8:
time: 227 us
  Pallas kernels  226 us (100%)
    pallas_call x1, Pallas kernels, local(): pl.pallas_call(kernel, out_shape=(pltpu.VMEM(weight.shape, bf16), pltpu.V...  222 us

profile of v8, /device:TPU:0, one launch (start us, length us, event | category | flops | bytes accessed | tf_op | source)
XLA Modules:
  0.0 227.0 jit_solution(8759779484125722333)
XLA Ops:
  0.6 222.3 %shard_map.67 = (bf16[1,4096,512]{2,1,0:T(8,128)(2,1)S(1)}, bf16[1,4096,512]{2,1,0:T(8,128)(2,1)S(1)}, bf16[2,128,4096]{2,1,0:T(8,128)(2,1)S(1)}) custom-call(bf16[1,4096,512]{2,1,0:T(8,128)(2,1)} %w_hbm.1, bf16[1,4096,512]{2,1,0:T(8,128)(2,1)} %m_hbm.1, bf16[2,128,4096]{2,1,0:T(8,128)(2,1)} %x_hbm.1, bf16[2,512,512]{2,1,0:T(8,128)(2,1)} %og_hbm.1), custom_call_target="tpu_custom_call" | custom-call | tf_op jit(solution)/shard_map/pallas_call | solution.py:460
  223.0 4.0 %shard_map.68 = (bf16[1,4096,512]{2,1,0:T(8,128)(2,1)}, bf16[1,4096,512]{2,1,0:T(8,128)(2,1)}, bf16[2,128,4096]{2,1,0:T(8,128)(2,1)}) custom-call(bf16[1,4096,512]{2,1,0:T(8,128)(2,1)S(1)} %get-tuple-element.6.w_in, bf16[1,4096,512]{2,1,0:T(8,128)(2,1)S(1)} %get-tuple-element.7.m_in, bf16[2,128,4096]{2,1,0:T(8,128)(2,1)S(1)} %get-tuple-element.8.g_in), custom_call_target="tpu_custom_call" | custom-call | tf_op jit(solution)/shard_map/pallas_call | solution.py:479
